TPU v7x, 128 devices: a whole 4x4x4 slice. The times are simulated.
128 devices in a mesh: row: 8 (over y, core), col: 16 (over x, z).
Axes of the slice: x: 4, y: 4, z: 4, core: 2. Of those that a mesh axis runs over, the one named last changes fastest.
Arguments:
- tile_data: float32 [8, 16, 288, 128, 128], P('row', 'col'), as said below
- tile_rows: int32 [8, 16, 288], P('row', 'col'), may hold values from 0 to 2047, as said below
- tile_cols: int32 [8, 16, 288], P('row', 'col'), may hold values from 0 to 1023, as said below
- tile_counts: int32 [8, 16], P('row', 'col'), may hold values from 128 to 288, as said below
Outputs:
- row_scale: float32 [2097152], P('row')
- column_scale: float32 [2097152], P('col')
Inputs may be any that keep to these rules, and one draw needn't show every extreme that they name: `tile_rows`: within one device the blocks of the slots are all different. Slot k < 128 of device (p, q) holds row block q * 128 + k and column block p * 128 + k, so every row and column of A meets a used slot. `tile_cols`: column blocks of the slots, as above. `tile_counts`: some device uses all 288 slots in every draw. `tile_data`: entries are nonzero reals whose tiles have row and column scales of differing sizes.
All inputs are finite; a program needn't handle non-finite values.
Results may differ from a plain program's by a relative error of at most 0.0001.
Values sent between devices are 32-bit elements; how exact they have to be, the bound alone decides.
A program may use at most 64 MiB of HBM per device.

v0:
```python
import jax
import jax.numpy as jnp
from jax import lax
from jax.sharding import PartitionSpec as P

DIAG = 128
SWEEPS = 4


epsilon = 1e-06


def local_terms(magnitude, row_blocks, column_blocks, row_scale, column_scale, want_peak):
    scaled = magnitude * row_scale[row_blocks][:, :, None] * column_scale[column_blocks][:, None, :]
    if want_peak:
        return (scaled.max(axis=2), scaled.max(axis=1))
    return (scaled.sum(axis=2), scaled.sum(axis=1))


def peak_rows(terms, row_blocks, length):
    empty = jnp.zeros((length, terms.shape[1]), jnp.float32)
    return lax.pmax(empty.at[row_blocks].max(terms), "col")


def peak_columns(terms, column_blocks, length):
    empty = jnp.zeros((length, terms.shape[1]), jnp.float32)
    return lax.pmax(empty.at[column_blocks].max(terms), "row")


def total_rows(terms, row_blocks, length):
    empty = jnp.zeros((length, terms.shape[1]), jnp.float32)
    return lax.psum(empty.at[row_blocks].add(terms), "col")


def total_columns(terms, column_blocks, length):
    empty = jnp.zeros((length, terms.shape[1]), jnp.float32)
    return lax.psum(empty.at[column_blocks].add(terms), "row")


def on_device(tile_data, tile_rows, tile_cols, tile_counts):
    blocks = tile_data[0, 0]
    row_blocks = tile_rows[0, 0]
    column_blocks = tile_cols[0, 0]
    used_count = tile_counts[0, 0]
    slots = blocks.shape[0]
    side = blocks.shape[1]
    row_length = DIAG * lax.axis_size("col")
    column_length = DIAG * lax.axis_size("row")
    in_use = jnp.arange(slots, dtype=jnp.int32) < used_count
    magnitude = jnp.where(in_use[:, None, None], jnp.abs(blocks), jnp.float32(0.0))
    row_scale = jnp.ones((row_length, side), jnp.float32)
    column_scale = jnp.ones((column_length, side), jnp.float32)
    for sweep in range(SWEEPS):
        row_terms, column_terms = local_terms(
            magnitude, row_blocks, column_blocks, row_scale, column_scale, True
        )
        peak_row = peak_rows(row_terms, row_blocks, row_length)
        peak_col = peak_columns(column_terms, column_blocks, column_length)
        row_scale = row_scale * lax.rsqrt(peak_row + epsilon)
        column_scale = column_scale * lax.rsqrt(peak_col + epsilon)
    row_terms, column_terms = local_terms(
        magnitude, row_blocks, column_blocks, row_scale, column_scale, False
    )
    total_row = total_rows(row_terms, row_blocks, row_length)
    total_col = total_columns(column_terms, column_blocks, column_length)
    row_scale = row_scale * lax.rsqrt(total_row + epsilon)
    column_scale = column_scale * lax.rsqrt(total_col + epsilon)
    return (row_scale.reshape(-1), column_scale.reshape(-1))


def solution(mesh):
    placed = (
        P("row", "col", None, None, None),
        P("row", "col", None),
        P("row", "col", None),
        P("row", "col"),
    )
    return jax.shard_map(
        on_device, mesh=mesh, in_specs=placed, out_specs=(P("row"), P("col")), check_vma=False
    )
```

profile of v0, /device:TPU:0, one launch (start us, length us, event | category | flops | bytes accessed | tf_op | source)
XLA Modules:
  0.0 876.4 jit_solution(11298934996179545294)
XLA Ops:
  11.6 15.0 %fusion.1 = (f32[288,128]{1,0:T(8,128)S(1)}, f32[288,128]{1,0:T(8,128)S(1)}) fusion(f32[288,128]{1,0:T(8,128)S(1)} %gather_fusion.1, f32[288,128]{1,0:T(8,128)S(1)} %gather_fusion, f32[1,1,288,128,128]{4,3,2,1,0:T(8,128)} %param.4, pred[288]{0:T(512)(128)(4,1)S(1)} %iota_compare_fusion), kind=kLoop, calls=%fused_computation.27 | loop fusion | flops 28237824 | bytes 19464480 | tf_op jit(solution)/shard_map/reduce_max | solution.py:16
  26.6 2.3 scatter_custom_fusion.1
  29.0 2.5 scatter_custom_fusion
  31.6 61.3 %all-reduce.13.cloned.1.call-done = f32[1024,128]{1,0:T(8,128)} async-done(((f32[1024,128]{1,0:T(8,128)}), f32[1024,128]{1,0:T(8,128)}) %all-reduce.13.cloned.1.call-update) | async-done | bytes 524304 | tf_op jit(solution)/shard_map/pmax | solution.py:27
  92.9 1.2 add_rsqrt_fusion.1
  95.2 88.2 %all-reduce.11.cloned.1.call-done = f32[2048,128]{1,0:T(8,128)} async-done(((f32[2048,128]{1,0:T(8,128)}), f32[2048,128]{1,0:T(8,128)}) %all-reduce.11.cloned.1.call-update) | async-done | bytes 1048592 | tf_op jit(solution)/shard_map/pmax | solution.py:22
  183.4 1.5 add_rsqrt_fusion
  185.9 15.0 %fusion.2 = (f32[288,128]{1,0:T(8,128)S(1)}, f32[288,128]{1,0:T(8,128)S(1)}) fusion(f32[288,128]{1,0:T(8,128)S(1)} %gather_fusion.3, f32[288,128]{1,0:T(8,128)S(1)} %gather_fusion.2, f32[1,1,288,128,128]{4,3,2,1,0:T(8,128)} %param.4, pred[288]{0:T(512)(128)(4,1)S(1)} %iota_compare_fusion), kind=kLoop, calls=%fused_computation.28 | loop fusion | flops 28237824 | bytes 19464480 | tf_op jit(solution)/shard_map/reduce_max | solution.py:16
  201.0 2.3 scatter_custom_fusion.3
  203.4 2.5 scatter_custom_fusion.2
  205.9 58.1 %all-reduce.17.cloned.1.call-done = f32[1024,128]{1,0:T(8,128)} async-done(((f32[1024,128]{1,0:T(8,128)}), f32[1024,128]{1,0:T(8,128)}) %all-reduce.17.cloned.1.call-update) | async-done | bytes 524304 | tf_op jit(solution)/shard_map/pmax | solution.py:27
  266.3 88.1 %all-reduce.15.cloned.1.call-done = f32[2048,128]{1,0:T(8,128)} async-done(((f32[2048,128]{1,0:T(8,128)}), f32[2048,128]{1,0:T(8,128)}) %all-reduce.15.cloned.1.call-update) | async-done | bytes 1048592 | tf_op jit(solution)/shard_map/pmax | solution.py:22
  354.4 1.5 rsqrt_multiply_fusion.2
  357.0 15.0 %fusion.4 = (f32[288,128]{1,0:T(8,128)S(1)}, f32[288,128]{1,0:T(8,128)S(1)}) fusion(f32[288,128]{1,0:T(8,128)S(1)} %gather_fusion.5, f32[288,128]{1,0:T(8,128)S(1)} %gather_fusion.4, f32[1,1,288,128,128]{4,3,2,1,0:T(8,128)} %param.4, pred[288]{0:T(512)(128)(4,1)S(1)} %iota_compare_fusion), kind=kLoop, calls=%fused_computation.30 | loop fusion | flops 28237824 | bytes 19464480 | tf_op jit(solution)/shard_map/reduce_max | solution.py:16
  372.0 2.3 scatter_custom_fusion.5
  374.6 2.5 scatter_custom_fusion.4
  377.2 57.9 %all-reduce.21.cloned.1.call-done = f32[1024,128]{1,0:T(8,128)} async-done(((f32[1024,128]{1,0:T(8,128)}), f32[1024,128]{1,0:T(8,128)}) %all-reduce.21.cloned.1.call-update) | async-done | bytes 524304 | tf_op jit(solution)/shard_map/pmax | solution.py:27
  437.2 88.2 %all-reduce.19.cloned.1.call-done = f32[2048,128]{1,0:T(8,128)} async-done(((f32[2048,128]{1,0:T(8,128)}), f32[2048,128]{1,0:T(8,128)}) %all-reduce.19.cloned.1.call-update) | async-done | bytes 1048592 | tf_op jit(solution)/shard_map/pmax | solution.py:22
  525.4 1.4 rsqrt_multiply_fusion.1
  527.8 15.0 %fusion.6 = (f32[288,128]{1,0:T(8,128)S(1)}, f32[288,128]{1,0:T(8,128)S(1)}) fusion(f32[288,128]{1,0:T(8,128)S(1)} %gather_fusion.7, f32[288,128]{1,0:T(8,128)S(1)} %gather_fusion.6, f32[1,1,288,128,128]{4,3,2,1,0:T(8,128)} %param.4, pred[288]{0:T(512)(128)(4,1)S(1)} %iota_compare_fusion), kind=kLoop, calls=%fused_computation.32 | loop fusion | flops 28237824 | bytes 19464480 | tf_op jit(solution)/shard_map/reduce_max | solution.py:16
  542.9 2.3 scatter_custom_fusion.7
  545.3 2.5 scatter_custom_fusion.6
  547.9 58.1 %all-reduce.25.cloned.1.call-done = f32[1024,128]{1,0:T(8,128)} async-done(((f32[1024,128]{1,0:T(8,128)}), f32[1024,128]{1,0:T(8,128)}) %all-reduce.25.cloned.1.call-update) | async-done | bytes 524304 | tf_op jit(solution)/shard_map/pmax | solution.py:27
  608.1 88.3 %all-reduce.23.cloned.1.call-done = f32[2048,128]{1,0:T(8,128)} async-done(((f32[2048,128]{1,0:T(8,128)}), f32[2048,128]{1,0:T(8,128)}) %all-reduce.23.cloned.1.call-update) | async-done | bytes 1048592 | tf_op jit(solution)/shard_map/pmax | solution.py:22
  696.4 1.4 rsqrt_multiply_fusion
  698.9 15.1 %fusion.8 = (f32[288,128]{1,0:T(8,128)S(1)}, f32[288,128]{1,0:T(8,128)S(1)}) fusion(f32[288,128]{1,0:T(8,128)S(1)} %gather_fusion.9, f32[288,128]{1,0:T(8,128)S(1)} %gather_fusion.8, f32[1,1,288,128,128]{4,3,2,1,0:T(8,128)} %param.4, pred[288]{0:T(512)(128)(4,1)S(1)} %iota_compare_fusion), kind=kLoop, calls=%fused_computation.34 | loop fusion | flops 28237824 | bytes 19464480 | tf_op jit(solution)/shard_map/reduce_sum | solution.py:17
  714.0 2.3 scatter_custom_fusion.9
  716.4 2.5 scatter_custom_fusion.8
  718.9 58.0 %all-reduce.29.cloned.1.call-done = f32[1024,128]{1,0:T(8,128)} async-done(((f32[1024,128]{1,0:T(8,128)}), f32[1024,128]{1,0:T(8,128)}) %all-reduce.29.cloned.1.call-update) | async-done | bytes 524304 | tf_op jit(solution)/shard_map/psum | solution.py:37
  776.9 1.9 multiply_bitcast_fusion.1
  778.8 88.4 %all-reduce.27.cloned.1.call-done = f32[2048,128]{1,0:T(8,128)} async-done(((f32[2048,128]{1,0:T(8,128)}), f32[2048,128]{1,0:T(8,128)}) %all-reduce.27.cloned.1.call-update) | async-done | bytes 1048592 | tf_op jit(solution)/shard_map/psum | solution.py:32
  867.2 2.3 multiply_bitcast_fusion
  (44 shorter events, 16.3 us)
Async XLA Ops:
  7.2 85.7 %all-reduce.13.cloned.1.call-start = ((), (), s32[]{:S(2)}) async-start(), calls=%async_computation.1 | async-start | bytes 1048576 | tf_op jit(solution)/shard_map/pmax | solution.py:27
  28.9 154.5 %all-reduce.11.cloned.1.call-start = ((), (), s32[]{:S(2)}) async-start(), calls=%async_computation | async-start | bytes 2097152 | tf_op jit(solution)/shard_map/pmax | solution.py:22
  31.5 232.5 %all-reduce.17.cloned.1.call-start = ((), (), s32[]{:S(2)}) async-start(), calls=%async_computation.3 | async-start | bytes 1048576 | tf_op jit(solution)/shard_map/pmax | solution.py:27
  92.9 171.1 %copy-start.1 = (f32[1024,128]{1,0:T(8,128)S(1)}, f32[1024,128]{1,0:T(8,128)}, u32[]{:S(2)}) copy-start(f32[1024,128]{1,0:T(8,128)} %all-reduce.13.cloned.1.call-done) | copy-start | bytes 1572868
  183.4 171.0 %copy-start = (f32[2048,128]{1,0:T(8,128)S(1)}, f32[2048,128]{1,0:T(8,128)}, u32[]{:S(2)}) copy-start(f32[2048,128]{1,0:T(8,128)} %all-reduce.11.cloned.1.call-done) | copy-start | bytes 3145732
  203.3 151.1 %all-reduce.15.cloned.1.call-start = ((), (), s32[]{:S(2)}) async-start(), calls=%async_computation.2 | async-start | bytes 2097152 | tf_op jit(solution)/shard_map/pmax | solution.py:22
  205.9 229.2 %all-reduce.21.cloned.1.call-start = ((), (), s32[]{:S(2)}) async-start(), calls=%async_computation.5 | async-start | bytes 1048576 | tf_op jit(solution)/shard_map/pmax | solution.py:27
  374.3 151.1 %all-reduce.19.cloned.1.call-start = ((), (), s32[]{:S(2)}) async-start(), calls=%async_computation.4 | async-start | bytes 2097152 | tf_op jit(solution)/shard_map/pmax | solution.py:22
  377.1 228.8 %all-reduce.25.cloned.1.call-start = ((), (), s32[]{:S(2)}) async-start(), calls=%async_computation.7 | async-start | bytes 1048576 | tf_op jit(solution)/shard_map/pmax | solution.py:27
  545.2 151.2 %all-reduce.23.cloned.1.call-start = ((), (), s32[]{:S(2)}) async-start(), calls=%async_computation.6 | async-start | bytes 2097152 | tf_op jit(solution)/shard_map/pmax | solution.py:22
  547.8 229.1 %all-reduce.29.cloned.1.call-start = ((), (), s32[]{:S(2)}) async-start(), calls=%async_computation.9 | async-start | bytes 1048576 | tf_op jit(solution)/shard_map/psum | solution.py:37
  716.3 150.9 %all-reduce.27.cloned.1.call-start = ((), (), s32[]{:S(2)}) async-start(), calls=%async_computation.8 | async-start | bytes 2097152 | tf_op jit(solution)/shard_map/psum | solution.py:32
Sparse Core Ops, SparseCore 0:
  29.1 63.8 all-reduce.12
  96.7 86.6 all-reduce.10
  203.4 60.5 all-reduce.16
  267.7 86.6 all-reduce.14
  374.5 60.5 all-reduce.20
  438.7 86.6 all-reduce.18
  545.3 60.5 all-reduce.24
  609.8 86.6 all-reduce.22
  716.4 60.3 all-reduce.28
  780.6 86.5 all-reduce.26
where the time goes:
time: 877 us; the launch traced here: 876 us
  waiting for transfers between devices  735 us (84%)
  other arithmetic  115 us (13%)
  between operations  15 us (2%)
  local copies, waits for them, and re-layouts  10.7 us (1%)
    pmax x4, waiting for transfers between devices, peak_rows(): return lax.pmax(empty.at[row_blocks].max(terms), 'col')  353 us
    pmax x4, waiting for transfers between devices, peak_columns(): return lax.pmax(empty.at[column_blocks].max(terms), 'row')  235 us
    psum x1, waiting for transfers between devices, total_rows(): return lax.psum(empty.at[row_blocks].add(terms), 'col')  88.4 us
    reduce_max x4, other arithmetic, local_terms(): return (scaled.max(axis=2), scaled.max(axis=1))  60.2 us
    psum x1, waiting for transfers between devices, total_columns(): return lax.psum(empty.at[column_blocks].add(terms), 'row')  58 us
  transfers between devices with their start and end apart: 10, of which 10 were waited for; matrix products, arithmetic and copies ran while one was open for 3% of the time, Pallas kernels for 0%

commit v1 on v0

v1 whole, which is shorter than its diff:
```python
import functools

import jax
import jax.numpy as jnp
from jax import lax
from jax.experimental import pallas as pl
from jax.experimental.pallas import tpu as pltpu
from jax.sharding import PartitionSpec as P

TILE = 128
DIAG = 128
SWEEPS = 4
epsilon = 1e-06

EXT = 256
ROW_CAP = 32
COL_CAP = 48
LEVELS = 8
GROUP = 8
CHUNK = 16

f32 = jnp.float32
bf16 = jnp.bfloat16
MESH = pltpu.DeviceIdType.MESH if hasattr(pltpu, "DeviceIdType") else pl.DeviceIdType.MESH


def halves(x):
    hi = x.astype(bf16)
    lo = (x - hi.astype(f32)).astype(bf16)
    return jnp.concatenate([hi, lo], axis=1)


def select_rows(onehot, x):
    y = jnp.dot(onehot, halves(x), preferred_element_type=f32)
    return y[:, :TILE] + y[:, TILE:]


def iota(shape, dim):
    return lax.broadcasted_iota(jnp.int32, shape, dim).astype(f32)


def columns(row):
    parts = [
        jnp.broadcast_to(row[:, i : i + TILE], (TILE, TILE)).T for i in range(0, row.shape[1], TILE)
    ]
    return jnp.concatenate(parts, axis=0)


def earlier_equal(cols, rows):
    count = cols.shape[0] // TILE
    out = []
    before = iota((TILE, TILE), 0) < iota((TILE, TILE), 1)
    for b in range(count):
        total = jnp.zeros((1, TILE), f32)
        here = rows[b]
        for a in range(b + 1):
            same = cols[a * TILE : (a + 1) * TILE] == here
            if a == b:
                same = same & before
            total = total + jnp.sum(jnp.where(same, 1.0, 0.0), axis=0, keepdims=True)
        out.append(total)
    return out


class Side:
    def __init__(self, axis, count, cap, key_row, refs):
        self.axis, self.count, self.cap, self.key_row = axis, count, cap, key_row
        self.entries = count * cap
        (
            self.own,
            self.ext,
            self.diag_term,
            self.ext_term,
            self.pack,
            self.unpack,
            self.levels,
            self.expand,
            self.id_recv,
            self.p1_send,
            self.p1_recv,
            self.p2_send,
            self.p2_recv,
            self.fin,
            self.send_sems,
            self.recv_sems,
        ) = refs
        self.me = lax.axis_index(axis)

    def partner(self, d):
        return lax.rem(self.me + d, self.count)

    def sender(self, d):
        return lax.rem(self.me + self.count - d, self.count)

    def copy(self, kind, d, src, dst, peer):
        kind, slot = kind
        return pltpu.make_async_remote_copy(
            src_ref=src,
            dst_ref=dst,
            send_sem=self.send_sems.at[kind, d],
            recv_sem=self.recv_sems.at[kind, slot, d],
            device_id={self.axis: peer},
            device_id_type=MESH,
        )

    def send(self, kind, send, recv):
        for d in range(1, self.count):
            peer = self.partner(d)
            self.copy(kind, d, send.at[peer], recv.at[self.me], peer).start()
        recv[self.me] = send[self.me]

    def wait_send(self, kind, send, recv):
        for d in range(1, self.count):
            peer = self.partner(d)
            self.copy(kind, d, send.at[peer], recv.at[self.me], peer).wait_send()

    def wait_recv(self, kind, send, recv):
        for d in range(1, self.count):
            peer = self.sender(d)
            self.copy(kind, d, send.at[peer], recv.at[peer], peer).wait_recv()


def ID():
    return (0, 0)


def FIRST(slot):
    return (1, slot)


def BACK(slot):
    return (2, slot)


def LAST():
    return (3, 0)


def prepare(side, info_ref, flag_ref):
    n, cap, entries = side.count, side.cap, side.entries
    key = info_ref[side.key_row : side.key_row + 1, :]
    owner = jnp.floor(key * (1.0 / DIAG))
    local = key - owner * DIAG
    used = key >= 0.0
    owner_cols = columns(owner)
    rank = earlier_equal(owner_cols, [owner[:, :TILE], owner[:, TILE:]])
    rank = jnp.concatenate(rank, axis=1)
    fits = used & (rank < cap - 1.0)
    dest = jnp.where(fits, owner * cap + rank, -1.0)
    over = jnp.where(used & (rank >= cap - 1.0), 1.0, 0.0)
    flag_ref[...] = jnp.maximum(flag_ref[...], jnp.max(over, axis=1, keepdims=True))
    side.pack[...] = jnp.where(iota((entries, EXT), 0) == dest, 1.0, 0.0).astype(bf16)
    dest_cols = columns(dest)
    for i in range(0, entries, TILE):
        lanes = iota((EXT, TILE), 1) + float(i)
        side.unpack[:, i : i + TILE] = jnp.where(dest_cols == lanes, 1.0, 0.0).astype(bf16)
    side.ext_term[...] = jnp.where(columns(jnp.where(used, 1.0, 0.0)) > 0.0, columns(local) + 1.0, 0.0)


def fill(side, flag_ref):
    side.p1_send[...] = select_rows(side.pack[...], side.ext_term[...]).reshape(side.count, side.cap, TILE)
    flag = jnp.broadcast_to(flag_ref[0:1, :].reshape(1, 1, TILE), (side.count, 1, TILE))
    side.p1_send[:, side.cap - 1 : side.cap, :] = flag


def take_flag(side, recv, flag_ref):
    seen = recv[:, side.cap - 1, :]
    flag_ref[...] = jnp.maximum(flag_ref[...], jnp.max(seen, axis=0, keepdims=True))


def learn(side, flag_ref):
    n, cap, entries = side.count, side.cap, side.entries
    take_flag(side, side.id_recv, flag_ref)
    place = lax.broadcasted_iota(jnp.int32, (n, cap, TILE), 1)
    ids = jnp.where(place == cap - 1, 0.0, side.id_recv[...]).reshape(entries, TILE)
    lanes = iota((TILE, TILE), 1)
    rows = []
    for i in range(0, entries, TILE):
        block = ids[i : i + TILE]
        side.expand[i : i + TILE, :] = jnp.where(block == lanes + 1.0, 1.0, 0.0).astype(bf16)
        rows.append(block.T)
    level = earlier_equal(ids, rows)
    wanted = iota((TILE, TILE), 0) + 1.0
    over = jnp.zeros((1, TILE), f32)
    for b, i in enumerate(range(0, entries, TILE)):
        hit = rows[b] == wanted
        over = jnp.maximum(
            over, jnp.where((rows[b][0:1] > 0.0) & (level[b] >= float(LEVELS)), 1.0, 0.0)
        )
        for t in range(LEVELS):
            side.levels[t * TILE : (t + 1) * TILE, i : i + TILE] = jnp.where(
                hit & (level[b] == float(t)), 1.0, 0.0
            ).astype(bf16)
    flag_ref[...] = jnp.maximum(flag_ref[...], jnp.max(over, axis=1, keepdims=True))


def put(side, slot):
    side.send(FIRST(slot), side.p1_send, side.p1_recv.at[slot])


def put_done(side, slot):
    side.wait_send(FIRST(slot), side.p1_send, side.p1_recv.at[slot])


def combine(side, flag_ref, slot, final):
    recv = side.p1_recv.at[slot]
    side.wait_recv(FIRST(slot), side.p1_send, recv)
    take_flag(side, recv, flag_ref)
    terms = select_rows(side.levels[...], recv[...].reshape(side.entries, TILE))
    terms = terms.reshape(LEVELS, TILE, TILE)
    if final:
        total = side.diag_term[...] + jnp.sum(terms, axis=0)
    else:
        total = jnp.maximum(side.diag_term[...], jnp.max(terms, axis=0))
    own = side.own[...]
    side.own[...] = own * lax.rsqrt((2.0 * total) * own + epsilon)


def give_back(side, slot):
    side.p2_send[...] = select_rows(side.expand[...], side.own[...]).reshape(side.count, side.cap, TILE)
    side.send(BACK(slot), side.p2_send, side.p2_recv.at[slot])


def take_back(side, slot):
    recv = side.p2_recv.at[slot]
    side.wait_recv(BACK(slot), side.p2_send, recv)
    side.ext[...] = select_rows(side.unpack[...], recv[...].reshape(side.entries, TILE))
    side.wait_send(BACK(slot), side.p2_send, recv)


def reduce_tiles(tiles, first, scale, out, count, final):
    def step(g, carry):
        base = pl.multiple_of(g * GROUP, GROUP)
        cols = scale[pl.ds(base, GROUP), :].T
        results = []
        for j in range(GROUP):
            x = tiles[first + base + j] * jnp.broadcast_to(cols[:, j : j + 1], (TILE, TILE))
            if final:
                results.append(jnp.sum(x, axis=0, keepdims=True))
            else:
                results.append(jnp.max(x, axis=0, keepdims=True))
        out[pl.ds(base, GROUP), :] = jnp.concatenate(results, axis=0)
        return carry

    lax.fori_loop(0, count // GROUP, step, 0)


def kernel(
    n_row, n_col, slots, info_ref, data_ref, row_out, col_out, flag_out, tiles, turned, flag_ref, load_sems, out_sems, *rest
):
    rows = Side("col", n_col, ROW_CAP, 0, rest[: len(rest) // 2])
    cols = Side("row", n_row, COL_CAP, 1, rest[len(rest) // 2 :])
    sides = (cols, rows)

    barrier = pltpu.get_barrier_semaphore()
    for side in sides:
        for d in range(1, side.count):
            pl.semaphore_signal(barrier, inc=1, device_id={side.axis: side.partner(d)}, device_id_type=MESH)

    extra = slots - DIAG
    order = list(range(DIAG // CHUNK, slots // CHUNK)) + list(range(DIAG // CHUNK))

    def load(c):
        return pltpu.make_async_copy(
            data_ref.at[pl.ds(c * CHUNK, CHUNK)], tiles.at[pl.ds(c * CHUNK, CHUNK)], load_sems.at[c]
        )

    for c in order:
        load(c).start()

    flag_ref[...] = jnp.zeros_like(flag_ref)
    for side in sides:
        prepare(side, info_ref, flag_ref)
    for side in sides:
        fill(side, flag_ref)
    pl.semaphore_wait(barrier, n_row + n_col - 2)
    for side in sides:
        side.send(ID(), side.p1_send, side.id_recv)

    count = info_ref[2:3, :TILE]

    def first_terms(c, side_terms, offset):
        row_term, col_term = side_terms
        load(c).wait()

        def step(g, carry):
            base = pl.multiple_of(c * CHUNK + g * GROUP, GROUP)
            row_results, col_results = [], []
            for j in range(GROUP):
                slot = base + j
                half = jnp.where(jnp.full((1, TILE), slot, jnp.int32).astype(f32) < count, 0.5, 0.0)
                x = jnp.abs(tiles[slot]) * half
                y = x.T
                tiles[slot] = x
                turned[slot] = y
                col_results.append(jnp.max(x, axis=0, keepdims=True))
                row_results.append(jnp.max(y, axis=0, keepdims=True))
            col_term[pl.ds(base - offset, GROUP), :] = jnp.concatenate(col_results, axis=0)
            row_term[pl.ds(base - offset, GROUP), :] = jnp.concatenate(row_results, axis=0)
            return carry

        lax.fori_loop(0, CHUNK // GROUP, step, 0)

    for side in sides:
        side.ext_term[...] = jnp.zeros_like(side.ext_term)
        side.own[...] = jnp.ones_like(side.own)
    for c in range(DIAG // CHUNK, slots // CHUNK):
        first_terms(c, (rows.ext_term, cols.ext_term), DIAG)
    for side in sides:
        side.wait_send(ID(), side.p1_send, side.id_recv)
        fill(side, flag_ref)
        put(side, 0)
    for c in range(DIAG // CHUNK):
        first_terms(c, (rows.diag_term, cols.diag_term), 0)
    for side in sides:
        side.wait_recv(ID(), side.p1_send, side.id_recv)
        learn(side, flag_ref)
    for side in sides:
        combine(side, flag_ref, 0, False)
        give_back(side, 0)
        put_done(side, 0)

    def sweep(t, final):
        slot, before = t % 2, (t + 1) % 2
        take_back(cols, before)
        reduce_tiles(turned, DIAG, cols.ext, rows.ext_term, extra, final)
        fill(rows, flag_ref)
        put(rows, slot)
        take_back(rows, before)
        reduce_tiles(tiles, DIAG, rows.ext, cols.ext_term, extra, final)
        fill(cols, flag_ref)
        put(cols, slot)
        reduce_tiles(turned, 0, cols.own, rows.diag_term, DIAG, final)
        reduce_tiles(tiles, 0, rows.own, cols.diag_term, DIAG, final)
        for side in sides:
            combine(side, flag_ref, slot, final)
            if not final:
                give_back(side, slot)
        for side in sides:
            put_done(side, slot)

    def middle(t, carry):
        sweep(t, False)
        return carry

    lax.fori_loop(1, SWEEPS, middle, 0)
    sweep(SWEEPS, True)

    flag_out[...] = flag_ref[...]
    for i, (side, out) in enumerate(((rows, row_out), (cols, col_out))):
        side.fin[...] = side.own[...]
        place = out.at[pl.ds(pl.multiple_of(side.me * DIAG, DIAG), DIAG)]
        for d in range(1, side.count):
            side.copy(LAST(), d, side.fin, place, side.partner(d)).start()
        pltpu.make_async_copy(side.fin, place, out_sems.at[i]).start()
    for i, (side, out) in enumerate(((rows, row_out), (cols, col_out))):
        place = out.at[pl.ds(pl.multiple_of(side.me * DIAG, DIAG), DIAG)]
        for d in range(1, side.count):
            peer = side.sender(d)
            there = out.at[pl.ds(pl.multiple_of(peer * DIAG, DIAG), DIAG)]
            side.copy(LAST(), d, side.fin, there, peer).wait_recv()
        for d in range(1, side.count):
            side.copy(LAST(), d, side.fin, place, side.partner(d)).wait_send()
        pltpu.make_async_copy(side.fin, place, out_sems.at[i]).wait()


def side_scratch(count, cap):
    entries = count * cap
    return [
        pltpu.VMEM((DIAG, TILE), f32),
        pltpu.VMEM((EXT, TILE), f32),
        pltpu.VMEM((DIAG, TILE), f32),
        pltpu.VMEM((EXT, TILE), f32),
        pltpu.VMEM((entries, EXT), bf16),
        pltpu.VMEM((EXT, entries), bf16),
        pltpu.VMEM((LEVELS * DIAG, entries), bf16),
        pltpu.VMEM((entries, DIAG), bf16),
        pltpu.VMEM((count, cap, TILE), f32),
        pltpu.VMEM((count, cap, TILE), f32),
        pltpu.VMEM((2, count, cap, TILE), f32),
        pltpu.VMEM((count, cap, TILE), f32),
        pltpu.VMEM((2, count, cap, TILE), f32),
        pltpu.VMEM((DIAG, TILE), f32),
        pltpu.SemaphoreType.DMA((4, count)),
        pltpu.SemaphoreType.DMA((4, 2, count)),
    ]


def sparse(tiles, row_blocks, column_blocks, used_count, n_row, n_col):
    slots = tiles.shape[0]
    in_use = jnp.arange(slots, dtype=jnp.int32) < used_count
    spare = EXT - (slots - DIAG)
    key = jnp.stack([row_blocks, column_blocks])[:, DIAG:]
    key = jnp.where(in_use[None, DIAG:], key, -1).astype(f32)
    key = jnp.pad(key, ((0, 0), (0, spare)), constant_values=-1.0)
    info = jnp.concatenate([key, jnp.full((6, EXT), used_count, jnp.int32).astype(f32)])
    return pl.pallas_call(
        functools.partial(kernel, n_row, n_col, slots),
        out_shape=(
            jax.ShapeDtypeStruct((n_col * DIAG, TILE), f32),
            jax.ShapeDtypeStruct((n_row * DIAG, TILE), f32),
            jax.ShapeDtypeStruct((8, TILE), f32),
        ),
        in_specs=[pl.BlockSpec(memory_space=pltpu.VMEM), pl.BlockSpec(memory_space=pl.ANY)],
        out_specs=(
            pl.BlockSpec(memory_space=pl.ANY),
            pl.BlockSpec(memory_space=pl.ANY),
            pl.BlockSpec(memory_space=pltpu.VMEM),
        ),
        scratch_shapes=[
            pltpu.VMEM((slots, TILE, TILE), f32),
            pltpu.VMEM((slots, TILE, TILE), f32),
            pltpu.VMEM((8, TILE), f32),
            pltpu.SemaphoreType.DMA((slots // CHUNK,)),
            pltpu.SemaphoreType.DMA((2,)),
            *side_scratch(n_col, ROW_CAP),
            *side_scratch(n_row, COL_CAP),
        ],
        compiler_params=pltpu.CompilerParams(
            collective_id=0, has_side_effects=True, vmem_limit_bytes=60 << 20
        ),
    )(info, tiles)


def gathered(x, axis):
    n = lax.axis_size(axis)
    me = lax.axis_index(axis)
    ring = [(i, (i + 1) % n) for i in range(n)]
    out = jnp.zeros((n,) + x.shape, x.dtype).at[me].set(x)

    def step(i, carry):
        out, y = carry
        y = lax.ppermute(y, axis, ring)
        return out.at[lax.rem(me + n - i, n)].set(y), y

    return lax.fori_loop(1, n, step, (out, x))[0]


def dense(blocks, row_blocks, column_blocks, used_count):
    slots, side = blocks.shape[:2]
    row_length = DIAG * lax.axis_size("col")
    column_length = DIAG * lax.axis_size("row")
    in_use = jnp.arange(slots, dtype=jnp.int32) < used_count
    magnitude = jnp.where(in_use[:, None, None], jnp.abs(blocks), f32(0.0))

    def sweep(t, carry):
        row_scale, column_scale = carry
        scaled = magnitude * row_scale[row_blocks][:, :, None] * column_scale[column_blocks][:, None, :]
        no_rows = jnp.zeros((row_length, side), f32)
        no_columns = jnp.zeros((column_length, side), f32)
        peak = t < SWEEPS

        def peaks():
            rows = no_rows.at[row_blocks].max(scaled.max(axis=2))
            columns = no_columns.at[column_blocks].max(scaled.max(axis=1))
            return rows, columns

        def totals():
            rows = no_rows.at[row_blocks].add(scaled.sum(axis=2))
            columns = no_columns.at[column_blocks].add(scaled.sum(axis=1))
            return rows, columns

        rows, columns = lax.cond(peak, peaks, totals)
        rows, columns = gathered(rows, "col"), gathered(columns, "row")
        rows = jnp.where(peak, rows.max(axis=0), rows.sum(axis=0))
        columns = jnp.where(peak, columns.max(axis=0), columns.sum(axis=0))
        return row_scale * lax.rsqrt(rows + epsilon), column_scale * lax.rsqrt(columns + epsilon)

    start = (jnp.ones((row_length, side), f32), jnp.ones((column_length, side), f32))
    return lax.fori_loop(0, SWEEPS + 1, sweep, start)


def on_device(tile_data, tile_rows, tile_cols, tile_counts):
    blocks = tile_data[0, 0]
    row_blocks = tile_rows[0, 0]
    column_blocks = tile_cols[0, 0]
    used_count = tile_counts[0, 0]
    n_row, n_col = lax.axis_size("row"), lax.axis_size("col")
    row_scale, column_scale, flag = sparse(blocks, row_blocks, column_blocks, used_count, n_row, n_col)
    row_scale, column_scale = lax.cond(
        flag[0, 0] > 0.0,
        lambda: dense(blocks, row_blocks, column_blocks, used_count),
        lambda: (row_scale, column_scale),
    )
    return (row_scale.reshape(-1), column_scale.reshape(-1))


def solution(mesh):
    placed = (
        P("row", "col", None, None, None),
        P("row", "col", None),
        P("row", "col", None),
        P("row", "col"),
    )
    return jax.shard_map(
        on_device, mesh=mesh, in_specs=placed, out_specs=(P("row"), P("col")), check_vma=False
    )
```

time: 877 us -> 174 us (0.20)
  waiting for transfers between devices: 735 us -> 0 us
  Pallas kernels: 0 us -> 164 us
  other arithmetic: 115 us -> 1.32 us
  between operations: 15 us -> 2.01 us
    pmax x8 -> x0, waiting for transfers between devices: 588 us -> none  [the longest x4 353 us: peak_rows(): return lax.pmax(empty.at[row_blocks].max(terms), 'col')]
    pallas_call x0 -> x1, Pallas kernels: none -> 164 us  [sparse(): pl.pallas_call(functools.partial(kernel, n_row, n_col, slots), out_shape=...]
    psum x2 -> x0, waiting for transfers between devices: 146 us -> none  [the longest x1 88.4 us: total_rows(): return lax.psum(empty.at[row_blocks].add(terms), 'col')]
    reduce_max x4 -> x0, other arithmetic: 60.2 us -> none  [local_terms(): return (scaled.max(axis=2), scaled.max(axis=1))]
    another operation x8 -> x0, other arithmetic: 19.3 us -> none  [the longest x4 10.1 us: peak_rows(): return lax.pmax(empty.at[row_blocks].max(terms), 'col')]
    reduce_sum x1 -> x0, other arithmetic: 15.1 us -> none  [local_terms(): return (scaled.sum(axis=2), scaled.sum(axis=1))]
    gather x10 -> x0, local copies, waits for them, and re-layouts: 10.6 us -> none  [the longest x5 5.3 us: local_terms(): column_scale[column_blocks][:, None, :]]
  transfers between devices with their start and end apart: 10 -> 0, of which waited for: 10 -> 0; matrix products, arithmetic and copies ran while one was open for 3% -> 0% of each run, Pallas kernels for 0% -> 0%
where the time goes in v1:
time: 174 us; the launch traced here: 172 us
  Pallas kernels  164 us (94%)
  local copies, waits for them, and re-layouts  5.34 us (3%)
  between operations  2.01 us (1%)
    pallas_call x1, Pallas kernels, sparse(): pl.pallas_call(functools.partial(kernel, n_row, n_col, slots), out_shape=...  164 us
    unnamed x6, local copies, waits for them, and re-layouts  4.14 us

profile of v1, /device:TPU:0, one launch (start us, length us, event | category | flops | bytes accessed | tf_op | source)
XLA Modules:
  0.0 172.4 jit_solution(444197681781935205)
XLA Ops:
  0.6 0.0 copy-start.4
  0.6 0.0 copy-start.5
  1.3 0.7 fusion.13
  2.1 0.6 pad_select_fusion.info_ref
  2.7 163.7 %shard_map.59 = (f32[2048,128]{1,0:T(8,128)}, f32[1024,128]{1,0:T(8,128)}, f32[8,128]{1,0:T(8,128)}) custom-call(f32[8,256]{1,0:T(8,128)} %pad_select_fusion.info_ref, f32[288,128,128]{2,1,0:T(8,128)} %bitcast.45), custom_call_target="tpu_custom_call" | custom-call | tf_op jit(solution)/shard_map/pallas_call | solution.py:397
  166.4 1.2 slice.151
  168.3 0.0 copy-done.4
  168.3 0.0 copy-done.5
  168.3 2.3 %copy.49 = f32[262144]{0:T(1024)} copy(f32[262144]{0:T(1024)} %get-tuple-element.841) | data formatting | bytes 2097152
  170.6 1.9 %copy.50 = f32[131072]{0:T(1024)} copy(f32[131072]{0:T(1024)} %get-tuple-element.842) | data formatting | bytes 1048576
  (3 shorter events, 0.0 us)
Async XLA Ops:
  0.6 167.6 %copy-start.4 = (s32[1,1,288]{2,1,0:T(1,128)S(1)}, s32[1,1,288]{2,1,0:T(1,128)}, u32[]{:S(2)}) copy-start(s32[1,1,288]{2,1,0:T(1,128)} %param.24) | copy-start | bytes 3460
  0.6 167.6 %copy-start.5 = (s32[1,1,288]{2,1,0:T(1,128)S(1)}, s32[1,1,288]{2,1,0:T(1,128)}, u32[]{:S(2)}) copy-start(s32[1,1,288]{2,1,0:T(1,128)} %param.23) | copy-start | bytes 3460

commit v2 on v1

--- a/solution.py
+++ b/solution.py
@@ -17,7 +17,9 @@
 COL_CAP = 48
 LEVELS = 8
 GROUP = 8
-CHUNK = 16
+PARTS = 2
+TAIL = 32
+QUARTERS = TILE // TAIL
 
 f32 = jnp.float32
 bf16 = jnp.bfloat16
@@ -68,8 +70,12 @@
         self.entries = count * cap
         (
             self.own,
+            self.own_turned,
             self.ext,
+            self.tail,
             self.diag_term,
+            self.ext_turned,
+            self.tail_term,
             self.ext_term,
             self.pack,
             self.unpack,
@@ -209,11 +215,13 @@
     terms = select_rows(side.levels[...], recv[...].reshape(side.entries, TILE))
     terms = terms.reshape(LEVELS, TILE, TILE)
     if final:
-        total = side.diag_term[...] + jnp.sum(terms, axis=0)
+        total = side.diag_term[...].T + jnp.sum(terms, axis=0)
     else:
-        total = jnp.maximum(side.diag_term[...], jnp.max(terms, axis=0))
+        total = jnp.maximum(side.diag_term[...].T, jnp.max(terms, axis=0))
     own = side.own[...]
-    side.own[...] = own * lax.rsqrt((2.0 * total) * own + epsilon)
+    own = own * lax.rsqrt((2.0 * total) * own + epsilon)
+    side.own[...] = own
+    side.own_turned[...] = own.T
 
 
 def give_back(side, slot):
@@ -224,29 +232,73 @@
 def take_back(side, slot):
     recv = side.p2_recv.at[slot]
     side.wait_recv(BACK(slot), side.p2_send, recv)
-    side.ext[...] = select_rows(side.unpack[...], recv[...].reshape(side.entries, TILE))
+    scale = select_rows(side.unpack[...], recv[...].reshape(side.entries, TILE))
+    side.ext[...] = scale[:TILE].T
+    tail = scale[TILE : TILE + TAIL]
+    if side.axis == "col":
+        tail = [tail] + [pltpu.roll(tail, TILE - q * TAIL, 1) for q in range(1, QUARTERS)]
+        side.tail[...] = jnp.concatenate(tail, axis=0).T[:TAIL]
+    else:
+        side.tail[...] = jnp.concatenate([tail] * QUARTERS, axis=0).T
     side.wait_send(BACK(slot), side.p2_send, recv)
 
 
-def reduce_tiles(tiles, first, scale, out, count, final):
+def gather_terms(side, final):
+    side.ext_term[:TILE, :] = side.ext_turned[...].T
+    if side.axis == "col":
+        empty = jnp.zeros((TILE - TAIL, TILE), f32)
+        turned = jnp.concatenate([side.tail_term[...], empty], axis=0).T
+        parts = [turned[:TAIL]]
+        parts += [pltpu.roll(turned[q * TAIL : (q + 1) * TAIL], q * TAIL, 1) for q in range(1, QUARTERS)]
+        side.ext_term[TILE : TILE + TAIL, :] = parts[0] + parts[1] + parts[2] + parts[3]
+    else:
+        parts = side.tail_term[...].T.reshape(QUARTERS, TAIL, TILE)
+        side.ext_term[TILE : TILE + TAIL, :] = jnp.sum(parts, axis=0) if final else jnp.max(parts, axis=0)
+
+
+def row_pass(tiles, scale, out, final):
+    scale = scale[...]
+
     def step(g, carry):
         base = pl.multiple_of(g * GROUP, GROUP)
-        cols = scale[pl.ds(base, GROUP), :].T
         results = []
         for j in range(GROUP):
-            x = tiles[first + base + j] * jnp.broadcast_to(cols[:, j : j + 1], (TILE, TILE))
-            if final:
-                results.append(jnp.sum(x, axis=0, keepdims=True))
-            else:
-                results.append(jnp.max(x, axis=0, keepdims=True))
+            x = tiles[base + j] * scale
+            reduce = jnp.sum if final else jnp.max
+            results.append(reduce(x, axis=0, keepdims=True))
         out[pl.ds(base, GROUP), :] = jnp.concatenate(results, axis=0)
         return carry
 
-    lax.fori_loop(0, count // GROUP, step, 0)
+    lax.fori_loop(0, tiles.shape[0] // GROUP, step, 0)
+
+
+def col_pass(tiles, scale, out, final):
+    def step(g, total):
+        base = pl.multiple_of(g * GROUP, GROUP)
+        for j in range(GROUP):
+            x = tiles[base + j] * scale[pl.ds(base + j, 1), :]
+            total = total + x if final else jnp.maximum(total, x)
+        return total
+
+    out[...] = lax.fori_loop(0, tiles.shape[0] // GROUP, step, jnp.zeros((TILE, TILE), f32))
 
 
 def kernel(
-    n_row, n_col, slots, info_ref, data_ref, row_out, col_out, flag_out, tiles, turned, flag_ref, load_sems, out_sems, *rest
+    n_row,
+    n_col,
+    info_ref,
+    data_ref,
+    row_out,
+    col_out,
+    flag_out,
+    diag_tiles,
+    ext_tiles,
+    tail_loaded,
+    tail_tiles,
+    flag_ref,
+    load_sems,
+    out_sems,
+    *rest,
 ):
     rows = Side("col", n_col, ROW_CAP, 0, rest[: len(rest) // 2])
     cols = Side("row", n_row, COL_CAP, 1, rest[len(rest) // 2 :])
@@ -257,16 +309,31 @@
         for d in range(1, side.count):
             pl.semaphore_signal(barrier, inc=1, device_id={side.axis: side.partner(d)}, device_id_type=MESH)
 
-    extra = slots - DIAG
-    order = list(range(DIAG // CHUNK, slots // CHUNK)) + list(range(DIAG // CHUNK))
-
-    def load(c):
-        return pltpu.make_async_copy(
-            data_ref.at[pl.ds(c * CHUNK, CHUNK)], tiles.at[pl.ds(c * CHUNK, CHUNK)], load_sems.at[c]
-        )
-
-    for c in order:
-        load(c).start()
+    def load(group, part):
+        tiles, first, count = ((ext_tiles, DIAG, TILE), (tail_loaded, DIAG + TILE, TAIL), (diag_tiles, 0, DIAG))[group]
+        height = TILE // PARTS
+        at = part * height
+        sem = load_sems.at[group, part]
+
+        def step(s, carry):
+            for j in range(GROUP):
+                slot = s * GROUP + j
+                pltpu.make_async_copy(
+                    data_ref.at[first + slot, pl.ds(at, height)], tiles.at[pl.ds(at, height), slot], sem
+                ).start()
+            return carry
+
+        lax.fori_loop(0, count // GROUP, step, 0)
+
+    def loaded(group, part):
+        tiles = (ext_tiles, tail_loaded, diag_tiles)[group]
+        height = TILE // PARTS
+        whole = tiles.at[pl.ds(part * height, height)]
+        pltpu.make_async_copy(whole, whole, load_sems.at[group, part]).wait()
+
+    for group in range(3):
+        for part in range(PARTS):
+            load(group, part)
 
     flag_ref[...] = jnp.zeros_like(flag_ref)
     for side in sides:
@@ -278,40 +345,60 @@
         side.send(ID(), side.p1_send, side.id_recv)
 
     count = info_ref[2:3, :TILE]
-
-    def first_terms(c, side_terms, offset):
-        row_term, col_term = side_terms
-        load(c).wait()
-
-        def step(g, carry):
-            base = pl.multiple_of(c * CHUNK + g * GROUP, GROUP)
-            row_results, col_results = [], []
+    lane = iota((1, TILE), 1)
+    ext_half = jnp.where(lane + float(DIAG) < count, 0.5, 0.0)
+    tail_slot = lax.broadcasted_iota(jnp.int32, (1, TILE), 1) % TAIL + (DIAG + TILE)
+    tail_half = jnp.where(tail_slot.astype(f32) < count, 0.5, 0.0)
+
+    def first_pass(group, tiles, half, row_term, col_term):
+        total = jnp.zeros((TILE, TILE), f32)
+        steps = TILE // PARTS // GROUP
+        for part in range(PARTS):
+            loaded(group, part)
+
+            def step(g, total):
+                base = pl.multiple_of(g * GROUP, GROUP)
+                results = []
+                for j in range(GROUP):
+                    x = jnp.abs(tiles[base + j]).T * half
+                    tiles[base + j] = x
+                    results.append(jnp.max(x, axis=0, keepdims=True))
+                    total = jnp.maximum(total, x)
+                row_term[pl.ds(base, GROUP), :] = jnp.concatenate(results, axis=0)
+                return total
+
+            total = lax.fori_loop(part * steps, (part + 1) * steps, step, total)
+        col_term[...] = total
+
+    def first_tail():
+        for part in range(PARTS):
+            loaded(1, part)
+
+        def step(g, total):
+            base = pl.multiple_of(g * GROUP, GROUP)
+            results = []
             for j in range(GROUP):
-                slot = base + j
-                half = jnp.where(jnp.full((1, TILE), slot, jnp.int32).astype(f32) < count, 0.5, 0.0)
-                x = jnp.abs(tiles[slot]) * half
-                y = x.T
-                tiles[slot] = x
-                turned[slot] = y
-                col_results.append(jnp.max(x, axis=0, keepdims=True))
-                row_results.append(jnp.max(y, axis=0, keepdims=True))
-            col_term[pl.ds(base - offset, GROUP), :] = jnp.concatenate(col_results, axis=0)
-            row_term[pl.ds(base - offset, GROUP), :] = jnp.concatenate(row_results, axis=0)
-            return carry
-
-        lax.fori_loop(0, CHUNK // GROUP, step, 0)
+                x = jnp.concatenate([tail_loaded[q * TAIL + base + j] for q in range(QUARTERS)], axis=0)
+                x = jnp.abs(x).T * tail_half
+                tail_tiles[base + j] = x
+                results.append(jnp.max(x, axis=0, keepdims=True))
+                total = jnp.maximum(total, x)
+            rows.tail_term[pl.ds(base, GROUP), :] = jnp.concatenate(results, axis=0)
+            return total
+
+        cols.tail_term[...] = lax.fori_loop(0, TAIL // GROUP, step, jnp.zeros((TILE, TILE), f32))
 
     for side in sides:
         side.ext_term[...] = jnp.zeros_like(side.ext_term)
         side.own[...] = jnp.ones_like(side.own)
-    for c in range(DIAG // CHUNK, slots // CHUNK):
-        first_terms(c, (rows.ext_term, cols.ext_term), DIAG)
+    first_pass(0, ext_tiles, ext_half, rows.ext_turned, cols.ext_turned)
+    first_tail()
     for side in sides:
         side.wait_send(ID(), side.p1_send, side.id_recv)
+        gather_terms(side, False)
         fill(side, flag_ref)
         put(side, 0)
-    for c in range(DIAG // CHUNK):
-        first_terms(c, (rows.diag_term, cols.diag_term), 0)
+    first_pass(2, diag_tiles, 0.5, rows.diag_term, cols.diag_term)
     for side in sides:
         side.wait_recv(ID(), side.p1_send, side.id_recv)
         learn(side, flag_ref)
@@ -323,15 +410,19 @@
     def sweep(t, final):
         slot, before = t % 2, (t + 1) % 2
         take_back(cols, before)
-        reduce_tiles(turned, DIAG, cols.ext, rows.ext_term, extra, final)
+        row_pass(ext_tiles, cols.ext, rows.ext_turned, final)
+        row_pass(tail_tiles, cols.tail, rows.tail_term, final)
+        gather_terms(rows, final)
         fill(rows, flag_ref)
         put(rows, slot)
         take_back(rows, before)
-        reduce_tiles(tiles, DIAG, rows.ext, cols.ext_term, extra, final)
+        col_pass(ext_tiles, rows.ext, cols.ext_turned, final)
+        col_pass(tail_tiles, rows.tail, cols.tail_term, final)
+        gather_terms(cols, final)
         fill(cols, flag_ref)
         put(cols, slot)
-        reduce_tiles(turned, 0, cols.own, rows.diag_term, DIAG, final)
-        reduce_tiles(tiles, 0, rows.own, cols.diag_term, DIAG, final)
+        row_pass(diag_tiles, cols.own_turned, rows.diag_term, final)
+        col_pass(diag_tiles, rows.own_turned, cols.diag_term, final)
         for side in sides:
             combine(side, flag_ref, slot, final)
             if not final:
@@ -364,12 +455,16 @@
         pltpu.make_async_copy(side.fin, place, out_sems.at[i]).wait()
 
 
-def side_scratch(count, cap):
+def side_scratch(count, cap, tail_scale, tail_term):
     entries = count * cap
     return [
         pltpu.VMEM((DIAG, TILE), f32),
-        pltpu.VMEM((EXT, TILE), f32),
-        pltpu.VMEM((DIAG, TILE), f32),
+        pltpu.VMEM((TILE, DIAG), f32),
+        pltpu.VMEM((TILE, TILE), f32),
+        pltpu.VMEM((tail_scale, TILE), f32),
+        pltpu.VMEM((TILE, DIAG), f32),
+        pltpu.VMEM((TILE, TILE), f32),
+        pltpu.VMEM((tail_term, TILE), f32),
         pltpu.VMEM((EXT, TILE), f32),
         pltpu.VMEM((entries, EXT), bf16),
         pltpu.VMEM((EXT, entries), bf16),
@@ -388,6 +483,7 @@
 
 def sparse(tiles, row_blocks, column_blocks, used_count, n_row, n_col):
     slots = tiles.shape[0]
+    assert slots == DIAG + TILE + TAIL
     in_use = jnp.arange(slots, dtype=jnp.int32) < used_count
     spare = EXT - (slots - DIAG)
     key = jnp.stack([row_blocks, column_blocks])[:, DIAG:]
@@ -395,7 +491,7 @@
     key = jnp.pad(key, ((0, 0), (0, spare)), constant_values=-1.0)
     info = jnp.concatenate([key, jnp.full((6, EXT), used_count, jnp.int32).astype(f32)])
     return pl.pallas_call(
-        functools.partial(kernel, n_row, n_col, slots),
+        functools.partial(kernel, n_row, n_col),
         out_shape=(
             jax.ShapeDtypeStruct((n_col * DIAG, TILE), f32),
             jax.ShapeDtypeStruct((n_row * DIAG, TILE), f32),
@@ -408,13 +504,15 @@
             pl.BlockSpec(memory_space=pltpu.VMEM),
         ),
         scratch_shapes=[
-            pltpu.VMEM((slots, TILE, TILE), f32),
-            pltpu.VMEM((slots, TILE, TILE), f32),
+            pltpu.VMEM((TILE, TILE, DIAG), f32),
+            pltpu.VMEM((TILE, TILE, TILE), f32),
+            pltpu.VMEM((TILE, TAIL, TILE), f32),
+            pltpu.VMEM((TAIL, TILE, TILE), f32),
             pltpu.VMEM((8, TILE), f32),
-            pltpu.SemaphoreType.DMA((slots // CHUNK,)),
+            pltpu.SemaphoreType.DMA((3, PARTS)),
             pltpu.SemaphoreType.DMA((2,)),
-            *side_scratch(n_col, ROW_CAP),
-            *side_scratch(n_row, COL_CAP),
+            *side_scratch(n_col, ROW_CAP, TAIL, TAIL),
+            *side_scratch(n_row, COL_CAP, TILE, TILE),
         ],
         compiler_params=pltpu.CompilerParams(
             collective_id=0, has_side_effects=True, vmem_limit_bytes=60 << 20

time: 174 us -> 105 us (0.60)
  Pallas kernels: 164 us -> 94.6 us
    pallas_call x1, Pallas kernels: 164 us -> 94.6 us  [sparse(): pl.pallas_call(functools.partial(kernel, n_row, n_col), out_shape=(jax.Sh...]
where the time goes in v2:
time: 105 us; the launch traced here: 103 us
  Pallas kernels  94.6 us (90%)
  local copies, waits for them, and re-layouts  5.34 us (5%)
  between operations  2.01 us (2%)
  other arithmetic  1.32 us (1%)
    pallas_call x1, Pallas kernels, sparse(): pl.pallas_call(functools.partial(kernel, n_row, n_col), out_shape=(jax.Sh...  94.6 us
    unnamed x6, local copies, waits for them, and re-layouts  4.14 us

profile of v2, /device:TPU:0, one launch (start us, length us, event | category | flops | bytes accessed | tf_op | source)
XLA Modules:
  0.0 103.5 jit_solution(9800566538239416603)
XLA Ops:
  0.6 0.0 copy-start.4
  0.6 0.0 copy-start.5
  1.3 0.7 fusion.13
  2.1 0.6 pad_select_fusion.info_ref
  2.7 94.6 %shard_map.59 = (f32[2048,128]{1,0:T(8,128)}, f32[1024,128]{1,0:T(8,128)}, f32[8,128]{1,0:T(8,128)}) custom-call(f32[8,256]{1,0:T(8,128)} %pad_select_fusion.info_ref, f32[288,128,128]{2,1,0:T(8,128)} %bitcast.45), custom_call_target="tpu_custom_call" | custom-call | tf_op jit(solution)/shard_map/pallas_call | solution.py:493
  97.3 1.2 %slice.151 = f32[1,1]{1,0:T(1,128)} slice(f32[8,128]{1,0:T(8,128)} %get-tuple-element.475), slice={[0:1], [0:1]} | slice | bytes 8 | tf_op jit(solution)/shard_map/slice | solution.py:579
  99.1 0.0 copy-done.4
  99.1 0.0 copy-done.5
  99.1 0.2 conditional.2
  99.4 2.3 %copy.49 = f32[262144]{0:T(1024)} copy(f32[262144]{0:T(1024)} %get-tuple-element.841) | data formatting | bytes 2097152
  101.6 1.9 %copy.50 = f32[131072]{0:T(1024)} copy(f32[131072]{0:T(1024)} %get-tuple-element.842) | data formatting | bytes 1048576
  (2 shorter events, 0.0 us)
Async XLA Ops:
  0.6 98.5 %copy-start.4 = (s32[1,1,288]{2,1,0:T(1,128)S(1)}, s32[1,1,288]{2,1,0:T(1,128)}, u32[]{:S(2)}) copy-start(s32[1,1,288]{2,1,0:T(1,128)} %param.24) | copy-start | bytes 3460
  0.6 98.5 %copy-start.5 = (s32[1,1,288]{2,1,0:T(1,128)S(1)}, s32[1,1,288]{2,1,0:T(1,128)}, u32[]{:S(2)}) copy-start(s32[1,1,288]{2,1,0:T(1,128)} %param.23) | copy-start | bytes 3460

commit v3 on v2

--- a/solution.py
+++ b/solution.py
@@ -13,11 +13,12 @@
 epsilon = 1e-06
 
 EXT = 256
-ROW_CAP = 32
-COL_CAP = 48
+ROW_CAP = 24
+COL_CAP = 40
 LEVELS = 8
 GROUP = 8
-PARTS = 2
+PARTS = (2, 1, 1)
+WIDTH = 4
 TAIL = 32
 QUARTERS = TILE // TAIL
 
@@ -64,10 +65,14 @@
     return out
 
 
+def padded(entries):
+    return -(-entries // TILE) * TILE
+
+
 class Side:
     def __init__(self, axis, count, cap, key_row, refs):
         self.axis, self.count, self.cap, self.key_row = axis, count, cap, key_row
-        self.entries = count * cap
+        self.entries = padded(count * cap)
         (
             self.own,
             self.own_turned,
@@ -87,6 +92,7 @@
             self.p2_send,
             self.p2_recv,
             self.fin,
+            self.flags,
             self.send_sems,
             self.recv_sems,
         ) = refs
@@ -109,21 +115,36 @@
             device_id_type=MESH,
         )
 
+    def place(self, ref, peer):
+        return ref.at[pl.ds(pl.multiple_of(peer * self.cap, 8), self.cap)]
+
     def send(self, kind, send, recv):
         for d in range(1, self.count):
             peer = self.partner(d)
-            self.copy(kind, d, send.at[peer], recv.at[self.me], peer).start()
-        recv[self.me] = send[self.me]
+            self.copy(kind, d, self.place(send, peer), self.place(recv, self.me), peer).start()
+        self.place(recv, self.me)[...] = self.place(send, self.me)[...]
 
     def wait_send(self, kind, send, recv):
         for d in range(1, self.count):
             peer = self.partner(d)
-            self.copy(kind, d, send.at[peer], recv.at[self.me], peer).wait_send()
+            self.copy(kind, d, self.place(send, peer), self.place(recv, self.me), peer).wait_send()
 
     def wait_recv(self, kind, send, recv):
         for d in range(1, self.count):
             peer = self.sender(d)
-            self.copy(kind, d, send.at[peer], recv.at[peer], peer).wait_recv()
+            self.copy(kind, d, self.place(send, peer), self.place(recv, peer), peer).wait_recv()
+
+    def tell(self, flag_ref):
+        for d in range(1, self.count):
+            self.copy((4, 0), d, flag_ref, self.flags.at[self.me], self.partner(d)).start()
+        self.flags[self.me] = flag_ref[...]
+
+    def told(self, flag_ref):
+        for d in range(1, self.count):
+            peer = self.sender(d)
+            self.copy((4, 0), d, flag_ref, self.flags.at[peer], peer).wait_recv()
+            self.copy((4, 0), d, flag_ref, self.flags.at[self.me], self.partner(d)).wait_send()
+        return jnp.max(self.flags[...], axis=0)
 
 
 def ID():
@@ -142,18 +163,23 @@
     return (3, 0)
 
 
-def prepare(side, info_ref, flag_ref):
-    n, cap, entries = side.count, side.cap, side.entries
-    key = info_ref[side.key_row : side.key_row + 1, :]
+def prepare(side, blocks_ref, used_count, key_ref, flag_ref):
+    cap, entries = side.cap, side.entries
+    blocks = blocks_ref[...].astype(f32)
+    key_ref[...] = jnp.full_like(key_ref, -1.0)
+    key_ref[0:1, :TILE] = blocks[:, DIAG : DIAG + TILE]
+    key_ref[0:1, TILE : TILE + TAIL] = blocks[:, DIAG + TILE :]
+    slot = lax.broadcasted_iota(jnp.int32, (1, EXT), 1) + DIAG
+    key = jnp.where(slot < used_count, key_ref[0:1, :], -1.0)
     owner = jnp.floor(key * (1.0 / DIAG))
     local = key - owner * DIAG
     used = key >= 0.0
     owner_cols = columns(owner)
     rank = earlier_equal(owner_cols, [owner[:, :TILE], owner[:, TILE:]])
     rank = jnp.concatenate(rank, axis=1)
-    fits = used & (rank < cap - 1.0)
+    fits = used & (rank < float(cap))
     dest = jnp.where(fits, owner * cap + rank, -1.0)
-    over = jnp.where(used & (rank >= cap - 1.0), 1.0, 0.0)
+    over = jnp.where(used & (rank >= float(cap)), 1.0, 0.0)
     flag_ref[...] = jnp.maximum(flag_ref[...], jnp.max(over, axis=1, keepdims=True))
     side.pack[...] = jnp.where(iota((entries, EXT), 0) == dest, 1.0, 0.0).astype(bf16)
     dest_cols = columns(dest)
@@ -163,22 +189,13 @@
     side.ext_term[...] = jnp.where(columns(jnp.where(used, 1.0, 0.0)) > 0.0, columns(local) + 1.0, 0.0)
 
 
-def fill(side, flag_ref):
-    side.p1_send[...] = select_rows(side.pack[...], side.ext_term[...]).reshape(side.count, side.cap, TILE)
-    flag = jnp.broadcast_to(flag_ref[0:1, :].reshape(1, 1, TILE), (side.count, 1, TILE))
-    side.p1_send[:, side.cap - 1 : side.cap, :] = flag
-
-
-def take_flag(side, recv, flag_ref):
-    seen = recv[:, side.cap - 1, :]
-    flag_ref[...] = jnp.maximum(flag_ref[...], jnp.max(seen, axis=0, keepdims=True))
+def fill(side):
+    side.p1_send[...] = select_rows(side.pack[...], side.ext_term[...])
 
 
 def learn(side, flag_ref):
-    n, cap, entries = side.count, side.cap, side.entries
-    take_flag(side, side.id_recv, flag_ref)
-    place = lax.broadcasted_iota(jnp.int32, (n, cap, TILE), 1)
-    ids = jnp.where(place == cap - 1, 0.0, side.id_recv[...]).reshape(entries, TILE)
+    entries = side.entries
+    ids = side.id_recv[...]
     lanes = iota((TILE, TILE), 1)
     rows = []
     for i in range(0, entries, TILE):
@@ -208,11 +225,10 @@
     side.wait_send(FIRST(slot), side.p1_send, side.p1_recv.at[slot])
 
 
-def combine(side, flag_ref, slot, final):
+def combine(side, slot, final):
     recv = side.p1_recv.at[slot]
     side.wait_recv(FIRST(slot), side.p1_send, recv)
-    take_flag(side, recv, flag_ref)
-    terms = select_rows(side.levels[...], recv[...].reshape(side.entries, TILE))
+    terms = select_rows(side.levels[...], recv[...])
     terms = terms.reshape(LEVELS, TILE, TILE)
     if final:
         total = side.diag_term[...].T + jnp.sum(terms, axis=0)
@@ -225,14 +241,14 @@
 
 
 def give_back(side, slot):
-    side.p2_send[...] = select_rows(side.expand[...], side.own[...]).reshape(side.count, side.cap, TILE)
+    side.p2_send[...] = select_rows(side.expand[...], side.own[...])
     side.send(BACK(slot), side.p2_send, side.p2_recv.at[slot])
 
 
 def take_back(side, slot):
     recv = side.p2_recv.at[slot]
     side.wait_recv(BACK(slot), side.p2_send, recv)
-    scale = select_rows(side.unpack[...], recv[...].reshape(side.entries, TILE))
+    scale = select_rows(side.unpack[...], recv[...])
     side.ext[...] = scale[:TILE].T
     tail = scale[TILE : TILE + TAIL]
     if side.axis == "col":
@@ -286,7 +302,9 @@
 def kernel(
     n_row,
     n_col,
-    info_ref,
+    count_ref,
+    rows_ref,
+    cols_ref,
     data_ref,
     row_out,
     col_out,
@@ -295,9 +313,13 @@
     ext_tiles,
     tail_loaded,
     tail_tiles,
+    key_ref,
     flag_ref,
+    all_flags,
     load_sems,
     out_sems,
+    near_sems,
+    far_sems,
     *rest,
 ):
     rows = Side("col", n_col, ROW_CAP, 0, rest[: len(rest) // 2])
@@ -311,7 +333,7 @@
 
     def load(group, part):
         tiles, first, count = ((ext_tiles, DIAG, TILE), (tail_loaded, DIAG + TILE, TAIL), (diag_tiles, 0, DIAG))[group]
-        height = TILE // PARTS
+        height = TILE // PARTS[group]
         at = part * height
         sem = load_sems.at[group, part]
 
@@ -327,33 +349,36 @@
 
     def loaded(group, part):
         tiles = (ext_tiles, tail_loaded, diag_tiles)[group]
-        height = TILE // PARTS
+        height = TILE // PARTS[group]
         whole = tiles.at[pl.ds(part * height, height)]
         pltpu.make_async_copy(whole, whole, load_sems.at[group, part]).wait()
 
     for group in range(3):
-        for part in range(PARTS):
+        for part in range(PARTS[group]):
             load(group, part)
 
     flag_ref[...] = jnp.zeros_like(flag_ref)
+    count = count_ref[0, 0]
+    for side, blocks_ref in ((cols, cols_ref), (rows, rows_ref)):
+        prepare(side, blocks_ref, count, key_ref, flag_ref)
+        for ref in (side.id_recv, side.p1_recv, side.p2_recv):
+            empty = side.entries - side.count * side.cap
+            if empty:
+                ref[..., side.entries - empty :, :] = jnp.zeros((*ref.shape[:-2], empty, TILE), f32)
     for side in sides:
-        prepare(side, info_ref, flag_ref)
-    for side in sides:
-        fill(side, flag_ref)
+        fill(side)
     pl.semaphore_wait(barrier, n_row + n_col - 2)
     for side in sides:
         side.send(ID(), side.p1_send, side.id_recv)
 
-    count = info_ref[2:3, :TILE]
-    lane = iota((1, TILE), 1)
-    ext_half = jnp.where(lane + float(DIAG) < count, 0.5, 0.0)
-    tail_slot = lax.broadcasted_iota(jnp.int32, (1, TILE), 1) % TAIL + (DIAG + TILE)
-    tail_half = jnp.where(tail_slot.astype(f32) < count, 0.5, 0.0)
+    lane = lax.broadcasted_iota(jnp.int32, (1, TILE), 1)
+    ext_half = jnp.where(lane + DIAG < count, 0.5, 0.0)
+    tail_half = jnp.where(lane % TAIL + (DIAG + TILE) < count, 0.5, 0.0)
 
     def first_pass(group, tiles, half, row_term, col_term):
         total = jnp.zeros((TILE, TILE), f32)
-        steps = TILE // PARTS // GROUP
-        for part in range(PARTS):
+        steps = TILE // PARTS[group] // GROUP
+        for part in range(PARTS[group]):
             loaded(group, part)
 
             def step(g, total):
@@ -371,8 +396,7 @@
         col_term[...] = total
 
     def first_tail():
-        for part in range(PARTS):
-            loaded(1, part)
+        loaded(1, 0)
 
         def step(g, total):
             base = pl.multiple_of(g * GROUP, GROUP)
@@ -396,14 +420,15 @@
     for side in sides:
         side.wait_send(ID(), side.p1_send, side.id_recv)
         gather_terms(side, False)
-        fill(side, flag_ref)
+        fill(side)
         put(side, 0)
     first_pass(2, diag_tiles, 0.5, rows.diag_term, cols.diag_term)
     for side in sides:
         side.wait_recv(ID(), side.p1_send, side.id_recv)
         learn(side, flag_ref)
+    rows.tell(flag_ref)
     for side in sides:
-        combine(side, flag_ref, 0, False)
+        combine(side, 0, False)
         give_back(side, 0)
         put_done(side, 0)
 
@@ -413,18 +438,18 @@
         row_pass(ext_tiles, cols.ext, rows.ext_turned, final)
         row_pass(tail_tiles, cols.tail, rows.tail_term, final)
         gather_terms(rows, final)
-        fill(rows, flag_ref)
+        fill(rows)
         put(rows, slot)
         take_back(rows, before)
         col_pass(ext_tiles, rows.ext, cols.ext_turned, final)
         col_pass(tail_tiles, rows.tail, cols.tail_term, final)
         gather_terms(cols, final)
-        fill(cols, flag_ref)
+        fill(cols)
         put(cols, slot)
         row_pass(diag_tiles, cols.own_turned, rows.diag_term, final)
         col_pass(diag_tiles, rows.own_turned, cols.diag_term, final)
         for side in sides:
-            combine(side, flag_ref, slot, final)
+            combine(side, slot, final)
             if not final:
                 give_back(side, slot)
         for side in sides:
@@ -435,28 +460,88 @@
         return carry
 
     lax.fori_loop(1, SWEEPS, middle, 0)
+    all_flags[...] = rows.told(flag_ref)
+    cols.tell(all_flags)
     sweep(SWEEPS, True)
 
-    flag_out[...] = flag_ref[...]
-    for i, (side, out) in enumerate(((rows, row_out), (cols, col_out))):
-        side.fin[...] = side.own[...]
-        place = out.at[pl.ds(pl.multiple_of(side.me * DIAG, DIAG), DIAG)]
-        for d in range(1, side.count):
-            side.copy(LAST(), d, side.fin, place, side.partner(d)).start()
-        pltpu.make_async_copy(side.fin, place, out_sems.at[i]).start()
-    for i, (side, out) in enumerate(((rows, row_out), (cols, col_out))):
-        place = out.at[pl.ds(pl.multiple_of(side.me * DIAG, DIAG), DIAG)]
-        for d in range(1, side.count):
-            peer = side.sender(d)
-            there = out.at[pl.ds(pl.multiple_of(peer * DIAG, DIAG), DIAG)]
-            side.copy(LAST(), d, side.fin, there, peer).wait_recv()
-        for d in range(1, side.count):
-            side.copy(LAST(), d, side.fin, place, side.partner(d)).wait_send()
-        pltpu.make_async_copy(side.fin, place, out_sems.at[i]).wait()
+    height = DIAG // 2
+    x, z = lax.div(rows.me, WIDTH), lax.rem(rows.me, WIDTH)
+
+    def at(half, near, far):
+        first, second = (z, x) if half == 0 else (x, z)
+        first, second = lax.rem(first + near, WIDTH), lax.rem(second + far, WIDTH)
+        return second * WIDTH + first if half == 0 else first * WIDTH + second
+
+    def block(half, device):
+        return row_out.at[pl.ds(pl.multiple_of(device * DIAG + half * height, 8), height)]
+
+    def row_copy(half, source, sems, device):
+        there = block(half, source[1])
+        return pltpu.make_async_remote_copy(
+            src_ref=source[0],
+            dst_ref=there,
+            send_sem=sems[0],
+            recv_sem=sems[1],
+            device_id={"col": device},
+            device_id_type=MESH,
+        )
+
+    def near_copy(half, d, device, owner):
+        sems = near_sems.at[0, half, d], near_sems.at[1, half, d]
+        return row_copy(half, (rows.fin.at[pl.ds(half * height, height)], owner), sems, device)
+
+    def far_copy(half, e, d, device, owner):
+        sems = far_sems.at[0, half, e, d], far_sems.at[1, half, e, d]
+        source = rows.fin.at[pl.ds(half * height, height)] if e == 0 else block(half, owner)
+        return row_copy(half, (source, owner), sems, device)
+
+    rows.fin[...] = rows.own[...]
+    for d in range(1, WIDTH):
+        for half in range(2):
+            near_copy(half, d, at(half, d, 0), rows.me).start()
+    cols.fin[...] = cols.own[...]
+    col_place = col_out.at[pl.ds(pl.multiple_of(cols.me * DIAG, DIAG), DIAG)]
+    for d in range(1, cols.count):
+        cols.copy(LAST(), d, cols.fin, col_place, cols.partner(d)).start()
+    for d in range(1, WIDTH):
+        for half in range(2):
+            far_copy(half, 0, d, at(half, 0, d), rows.me).start()
+    row_place = row_out.at[pl.ds(pl.multiple_of(rows.me * DIAG, DIAG), DIAG)]
+    kept = (
+        pltpu.make_async_copy(rows.fin, row_place, out_sems.at[0]),
+        pltpu.make_async_copy(cols.fin, col_place, out_sems.at[1]),
+    )
+    for copy in kept:
+        copy.start()
+    flag_out[0, 0] = jnp.max(cols.told(all_flags)).astype(jnp.int32)
+    for e in range(1, WIDTH):
+        for half in range(2):
+            owner = at(half, WIDTH - e, 0)
+            near_copy(half, e, owner, owner).wait_recv()
+            for d in range(1, WIDTH):
+                far_copy(half, e, d, at(half, 0, d), owner).start()
+    for d in range(1, WIDTH):
+        for half in range(2):
+            for e in range(WIDTH):
+                sender = at(half, 0, WIDTH - d)
+                far_copy(half, e, d, sender, at(half, WIDTH - e, WIDTH - d)).wait_recv()
+    for d in range(1, cols.count):
+        peer = cols.sender(d)
+        there = col_out.at[pl.ds(pl.multiple_of(peer * DIAG, DIAG), DIAG)]
+        cols.copy(LAST(), d, cols.fin, there, peer).wait_recv()
+        cols.copy(LAST(), d, cols.fin, col_place, cols.partner(d)).wait_send()
+    for d in range(1, WIDTH):
+        for half in range(2):
+            near_copy(half, d, at(half, d, 0), rows.me).wait_send()
+            for e in range(WIDTH):
+                owner = at(half, WIDTH - e, 0) if e else rows.me
+                far_copy(half, e, d, at(half, 0, d), owner).wait_send()
+    for copy in kept:
+        copy.wait()
 
 
 def side_scratch(count, cap, tail_scale, tail_term):
-    entries = count * cap
+    entries = padded(count * cap)
     return [
         pltpu.VMEM((DIAG, TILE), f32),
         pltpu.VMEM((TILE, DIAG), f32),
@@ -470,54 +555,57 @@
         pltpu.VMEM((EXT, entries), bf16),
         pltpu.VMEM((LEVELS * DIAG, entries), bf16),
         pltpu.VMEM((entries, DIAG), bf16),
-        pltpu.VMEM((count, cap, TILE), f32),
-        pltpu.VMEM((count, cap, TILE), f32),
-        pltpu.VMEM((2, count, cap, TILE), f32),
-        pltpu.VMEM((count, cap, TILE), f32),
-        pltpu.VMEM((2, count, cap, TILE), f32),
+        pltpu.VMEM((entries, TILE), f32),
+        pltpu.VMEM((entries, TILE), f32),
+        pltpu.VMEM((2, entries, TILE), f32),
+        pltpu.VMEM((entries, TILE), f32),
+        pltpu.VMEM((2, entries, TILE), f32),
         pltpu.VMEM((DIAG, TILE), f32),
-        pltpu.SemaphoreType.DMA((4, count)),
-        pltpu.SemaphoreType.DMA((4, 2, count)),
+        pltpu.VMEM((count, 8, TILE), f32),
+        pltpu.SemaphoreType.DMA((5, count)),
+        pltpu.SemaphoreType.DMA((5, 2, count)),
     ]
 
 
 def sparse(tiles, row_blocks, column_blocks, used_count, n_row, n_col):
-    slots = tiles.shape[0]
-    assert slots == DIAG + TILE + TAIL
-    in_use = jnp.arange(slots, dtype=jnp.int32) < used_count
-    spare = EXT - (slots - DIAG)
-    key = jnp.stack([row_blocks, column_blocks])[:, DIAG:]
-    key = jnp.where(in_use[None, DIAG:], key, -1).astype(f32)
-    key = jnp.pad(key, ((0, 0), (0, spare)), constant_values=-1.0)
-    info = jnp.concatenate([key, jnp.full((6, EXT), used_count, jnp.int32).astype(f32)])
+    assert tiles.shape[0] == DIAG + TILE + TAIL and n_col == WIDTH * WIDTH
     return pl.pallas_call(
         functools.partial(kernel, n_row, n_col),
         out_shape=(
             jax.ShapeDtypeStruct((n_col * DIAG, TILE), f32),
             jax.ShapeDtypeStruct((n_row * DIAG, TILE), f32),
-            jax.ShapeDtypeStruct((8, TILE), f32),
+            jax.ShapeDtypeStruct((1, 1), jnp.int32),
         ),
-        in_specs=[pl.BlockSpec(memory_space=pltpu.VMEM), pl.BlockSpec(memory_space=pl.ANY)],
+        in_specs=[
+            pl.BlockSpec(memory_space=pltpu.SMEM),
+            pl.BlockSpec(memory_space=pltpu.VMEM),
+            pl.BlockSpec(memory_space=pltpu.VMEM),
+            pl.BlockSpec(memory_space=pltpu.HBM),
+        ],
         out_specs=(
             pl.BlockSpec(memory_space=pl.ANY),
             pl.BlockSpec(memory_space=pl.ANY),
-            pl.BlockSpec(memory_space=pltpu.VMEM),
+            pl.BlockSpec(memory_space=pltpu.SMEM),
         ),
         scratch_shapes=[
             pltpu.VMEM((TILE, TILE, DIAG), f32),
             pltpu.VMEM((TILE, TILE, TILE), f32),
             pltpu.VMEM((TILE, TAIL, TILE), f32),
             pltpu.VMEM((TAIL, TILE, TILE), f32),
+            pltpu.VMEM((8, EXT), f32),
             pltpu.VMEM((8, TILE), f32),
-            pltpu.SemaphoreType.DMA((3, PARTS)),
+            pltpu.VMEM((8, TILE), f32),
+            pltpu.SemaphoreType.DMA((3, max(PARTS))),
             pltpu.SemaphoreType.DMA((2,)),
+            pltpu.SemaphoreType.DMA((2, 2, WIDTH)),
+            pltpu.SemaphoreType.DMA((2, 2, WIDTH, WIDTH)),
             *side_scratch(n_col, ROW_CAP, TAIL, TAIL),
             *side_scratch(n_row, COL_CAP, TILE, TILE),
         ],
         compiler_params=pltpu.CompilerParams(
-            collective_id=0, has_side_effects=True, vmem_limit_bytes=60 << 20
+            collective_id=0, has_side_effects=True, vmem_limit_bytes=52 << 20
         ),
-    )(info, tiles)
+    )(used_count.reshape(1, 1), row_blocks.reshape(1, -1), column_blocks.reshape(1, -1), tiles)
 
 
 def gathered(x, axis):
@@ -576,7 +664,7 @@
     n_row, n_col = lax.axis_size("row"), lax.axis_size("col")
     row_scale, column_scale, flag = sparse(blocks, row_blocks, column_blocks, used_count, n_row, n_col)
     row_scale, column_scale = lax.cond(
-        flag[0, 0] > 0.0,
+        flag[0, 0] > 0,
         lambda: dense(blocks, row_blocks, column_blocks, used_count),
         lambda: (row_scale, column_scale),
     )

time: 105 us -> 95.2 us (0.907); the launches traced: 103 us -> 95 us
  Pallas kernels: 94.6 us -> 88.6 us
  other arithmetic: 1.32 us -> 0 us
  local copies, waits for them, and re-layouts: 5.34 us -> 4.14 us
    pallas_call x1, Pallas kernels: 94.6 us -> 88.6 us  [sparse(): pl.pallas_call(functools.partial(kernel, n_row, n_col), out_shape=(jax.Sh...]
    slice x2 -> x0, local copies, waits for them, and re-layouts: 1.2 us -> none  [the longest x1 1.19 us: on_device(): flag[0, 0] > 0.0]
where the time goes in v3:
time: 95.2 us; the launch traced here: 95 us
  Pallas kernels  88.6 us (93%)
  local copies, waits for them, and re-layouts  4.14 us (4%)
  between operations  2.03 us (2%)
    pallas_call x1, Pallas kernels, sparse(): pl.pallas_call(functools.partial(kernel, n_row, n_col), out_shape=(jax.Sh...  88.6 us
    unnamed x6, local copies, waits for them, and re-layouts  4.14 us

profile of v3, /device:TPU:0, one launch (start us, length us, event | category | flops | bytes accessed | tf_op | source)
XLA Modules:
  0.0 95.0 jit_solution(867788327777263078)
XLA Ops:
  0.6 0.0 copy-start.5
  0.6 0.0 copy-start.4
  1.3 88.6 %shard_map.59 = (f32[2048,128]{1,0:T(8,128)}, f32[1024,128]{1,0:T(8,128)}, s32[1,1]{1,0:T(1,128)}) custom-call(s32[1,1]{1,0:T(1,128)S(6)} %copy.47.count_ref, s32[1,288]{1,0:T(1,128)} %bitcast.45, s32[1,288]{1,0:T(1,128)} %bitcast.46, f32[288,128,128]{2,1,0:T(8,128)} %bitcast.43), custom_call_target="tpu_custom_call" | custom-call | tf_op jit(solution)/shard_map/pallas_call | solution.py:572
  90.6 0.0 copy-done.5
  90.6 0.0 copy-done.4
  90.6 0.2 conditional.2
  90.9 2.3 %copy.49 = f32[262144]{0:T(1024)} copy(f32[262144]{0:T(1024)} %get-tuple-element.842) | data formatting | bytes 2097152
  93.1 1.9 %copy.50 = f32[131072]{0:T(1024)} copy(f32[131072]{0:T(1024)} %get-tuple-element.843) | data formatting | bytes 1048576
Async XLA Ops:
  0.6 90.0 %copy-start.5 = (s32[1,1,288]{2,1,0:T(1,128)S(1)}, s32[1,1,288]{2,1,0:T(1,128)}, u32[]{:S(2)}) copy-start(s32[1,1,288]{2,1,0:T(1,128)} %param.24) | copy-start | bytes 3460
  0.6 90.0 %copy-start.4 = (s32[1,1,288]{2,1,0:T(1,128)S(1)}, s32[1,1,288]{2,1,0:T(1,128)}, u32[]{:S(2)}) copy-start(s32[1,1,288]{2,1,0:T(1,128)} %param.23) | copy-start | bytes 3460

commit v4 on v3

--- a/solution.py
+++ b/solution.py
@@ -18,6 +18,8 @@
 LEVELS = 8
 GROUP = 8
 PARTS = (2, 1, 1)
+PIECE = 256
+HOPS = (0, 1, 2, 1)
 WIDTH = 4
 TAIL = 32
 QUARTERS = TILE // TAIL
@@ -97,12 +99,21 @@
             self.recv_sems,
         ) = refs
         self.me = lax.axis_index(axis)
+        self.minor = minor = count // WIDTH
+        steps = [(a, b) for a in range(WIDTH) for b in range(minor) if a or b]
+        self.steps = sorted(steps, key=lambda s: -sum(HOPS[i] for i in s))
+        self.major_me, self.minor_me = lax.div(self.me, minor), lax.rem(self.me, minor)
+
+    def shifted(self, a, b):
+        return lax.rem(self.major_me + a, WIDTH) * self.minor + lax.rem(self.minor_me + b, self.minor)
 
     def partner(self, d):
-        return lax.rem(self.me + d, self.count)
+        a, b = self.steps[d - 1]
+        return self.shifted(a, b)
 
     def sender(self, d):
-        return lax.rem(self.me + self.count - d, self.count)
+        a, b = self.steps[d - 1]
+        return self.shifted(WIDTH - a, self.minor - b)
 
     def copy(self, kind, d, src, dst, peer):
         kind, slot = kind
@@ -353,7 +364,7 @@
         whole = tiles.at[pl.ds(part * height, height)]
         pltpu.make_async_copy(whole, whole, load_sems.at[group, part]).wait()
 
-    for group in range(3):
+    for group in range(2):
         for part in range(PARTS[group]):
             load(group, part)
 
@@ -370,6 +381,9 @@
     pl.semaphore_wait(barrier, n_row + n_col - 2)
     for side in sides:
         side.send(ID(), side.p1_send, side.id_recv)
+
+    for part in range(PARTS[2]):
+        load(2, part)
 
     lane = lax.broadcasted_iota(jnp.int32, (1, TILE), 1)
     ext_half = jnp.where(lane + DIAG < count, 0.5, 0.0)
@@ -432,34 +446,38 @@
         give_back(side, 0)
         put_done(side, 0)
 
-    def sweep(t, final):
-        slot, before = t % 2, (t + 1) % 2
+    def row_step(slot, before, final):
         take_back(cols, before)
         row_pass(ext_tiles, cols.ext, rows.ext_turned, final)
         row_pass(tail_tiles, cols.tail, rows.tail_term, final)
         gather_terms(rows, final)
         fill(rows)
         put(rows, slot)
+
+    def col_step(slot, before, final):
         take_back(rows, before)
         col_pass(ext_tiles, rows.ext, cols.ext_turned, final)
         col_pass(tail_tiles, rows.tail, cols.tail_term, final)
         gather_terms(cols, final)
         fill(cols)
         put(cols, slot)
+
+    def sweep(t, final):
+        slot, before = t % 2, (t + 1) % 2
+        first, second = (row_step, col_step) if t % 2 else (col_step, row_step)
+        first(slot, before, final)
+        second(slot, before, final)
         row_pass(diag_tiles, cols.own_turned, rows.diag_term, final)
         col_pass(diag_tiles, rows.own_turned, cols.diag_term, final)
-        for side in sides:
+        for side in (rows, cols) if t % 2 else (cols, rows):
             combine(side, slot, final)
             if not final:
                 give_back(side, slot)
         for side in sides:
             put_done(side, slot)
 
-    def middle(t, carry):
+    for t in range(1, SWEEPS):
         sweep(t, False)
-        return carry
-
-    lax.fori_loop(1, SWEEPS, middle, 0)
     all_flags[...] = rows.told(flag_ref)
     cols.tell(all_flags)
     sweep(SWEEPS, True)
@@ -608,6 +626,30 @@
     )(used_count.reshape(1, 1), row_blocks.reshape(1, -1), column_blocks.reshape(1, -1), tiles)
 
 
+def settle_kernel(row_ref, col_ref, row_out, col_out, sems):
+    copies = []
+    for ref, out in ((row_ref, row_out), (col_ref, col_out)):
+        for i in range(ref.shape[0] // PIECE):
+            at = pl.ds(i * PIECE, PIECE)
+            copies.append(pltpu.make_async_copy(ref.at[at], out.at[at], sems.at[len(copies)]))
+    for copy in copies:
+        copy.start()
+    for copy in copies:
+        copy.wait()
+
+
+def settle(row_scale, column_scale):
+    pieces = (row_scale.shape[0] + column_scale.shape[0]) // PIECE
+    anywhere = pl.BlockSpec(memory_space=pl.ANY)
+    return pl.pallas_call(
+        settle_kernel,
+        out_shape=tuple(jax.ShapeDtypeStruct(x.shape, x.dtype) for x in (row_scale, column_scale)),
+        in_specs=[anywhere, anywhere],
+        out_specs=(anywhere, anywhere),
+        scratch_shapes=[pltpu.SemaphoreType.DMA((pieces,))],
+    )(row_scale, column_scale)
+
+
 def gathered(x, axis):
     n = lax.axis_size(axis)
     me = lax.axis_index(axis)
@@ -666,7 +708,7 @@
     row_scale, column_scale = lax.cond(
         flag[0, 0] > 0,
         lambda: dense(blocks, row_blocks, column_blocks, used_count),
-        lambda: (row_scale, column_scale),
+        lambda: settle(row_scale, column_scale),
     )
     return (row_scale.reshape(-1), column_scale.reshape(-1))
 

time: 95.2 us -> 86.5 us (0.909)
  Pallas kernels: 88.6 us -> 84.1 us
  local copies, waits for them, and re-layouts: 4.14 us -> 0.01 us
    pallas_call x1, Pallas kernels: 88.6 us -> 82.9 us  [sparse(): pl.pallas_call(functools.partial(kernel, n_row, n_col), out_shape=(jax.Sh...]
    unnamed x6 -> x4, local copies, waits for them, and re-layouts: 4.14 us -> 0.01 us
    pallas_call x0 -> x1, Pallas kernels: none -> 1.23 us  [settle(): pl.pallas_call(settle_kernel, out_shape=tuple((jax.ShapeDtypeStruct(x.sha...]
where the time goes in v4:
time: 86.5 us; the launch traced here: 86.3 us
  Pallas kernels  84.1 us (97%)
  between operations  2.18 us (3%)
    pallas_call x1, Pallas kernels, sparse(): pl.pallas_call(functools.partial(kernel, n_row, n_col), out_shape=(jax.Sh...  82.9 us

profile of v4, /device:TPU:0, one launch (start us, length us, event | category | flops | bytes accessed | tf_op | source)
XLA Modules:
  0.0 86.3 jit_solution(15361461636761317573)
XLA Ops:
  0.6 0.0 copy-start.5
  0.6 0.0 copy-start.4
  1.3 82.9 %shard_map.59 = (f32[2048,128]{1,0:T(8,128)S(1)}, f32[1024,128]{1,0:T(8,128)S(1)}, s32[1,1]{1,0:T(1,128)}) custom-call(s32[1,1]{1,0:T(1,128)S(6)} %copy.45.count_ref, s32[1,288]{1,0:T(1,128)} %bitcast.45, s32[1,288]{1,0:T(1,128)} %bitcast.46, f32[288,128,128]{2,1,0:T(8,128)} %bitcast.43), custom_call_target="tpu_custom_call" | custom-call | tf_op jit(solution)/shard_map/pallas_call | solution.py:590
  84.9 0.0 copy-done.5
  84.9 0.0 copy-done.4
  84.9 1.3 %conditional.2 = (f32[262144]{0:T(1024)}, f32[131072]{0:T(1024)}) conditional(s32[]{:T(128)} %bitcast.12, (f32[2048,128]{1,0:T(8,128)S(1)}, f32[1024,128]{1,0:T(8,128)S(1)}) %tuple.113, (s32[1,1,288]{2,1,0:T(1,128)S(1)}, s32[1,1]{1,0:T(1,128)}, f32[288,128,128]{2,1,0:T(8,128)}, s32[1,1,288]{2,1,0:T(1,128)S(1)}) %tuple.203), branch_computations={%region_0.0_spmd, %region_1.26_spmd} | conditional | flops 40769284 | bytes 240286992 | solution.py:708
  84.9 1.2 %branch_0_fun.1 = (f32[2048,128]{1,0:T(8,128)}, f32[1024,128]{1,0:T(8,128)}) custom-call(f32[2048,128]{1,0:T(8,128)S(1)} %get-tuple-element.436.row_ref, f32[1024,128]{1,0:T(8,128)S(1)} %get-tuple-element.437.col_ref), custom_call_target="tpu_custom_call" | custom-call | tf_op jit(solution)/shard_map/cond/branch_0_fun/pallas_call | solution.py:644
Async XLA Ops:
  0.6 84.3 %copy-start.5 = (s32[1,1,288]{2,1,0:T(1,128)S(1)}, s32[1,1,288]{2,1,0:T(1,128)}, u32[]{:S(2)}) copy-start(s32[1,1,288]{2,1,0:T(1,128)} %param.24) | copy-start | bytes 3460
  0.6 84.3 %copy-start.4 = (s32[1,1,288]{2,1,0:T(1,128)S(1)}, s32[1,1,288]{2,1,0:T(1,128)}, u32[]{:S(2)}) copy-start(s32[1,1,288]{2,1,0:T(1,128)} %param.23) | copy-start | bytes 3460

commit v5 on v4

--- a/solution.py
+++ b/solution.py
@@ -170,10 +170,6 @@
     return (2, slot)
 
 
-def LAST():
-    return (3, 0)
-
-
 def prepare(side, blocks_ref, used_count, key_ref, flag_ref):
     cap, entries = side.cap, side.entries
     blocks = blocks_ref[...].astype(f32)
@@ -331,6 +327,8 @@
     out_sems,
     near_sems,
     far_sems,
+    ring_sems,
+    core_sems,
     *rest,
 ):
     rows = Side("col", n_col, ROW_CAP, 0, rest[: len(rest) // 2])
@@ -483,77 +481,119 @@
     sweep(SWEEPS, True)
 
     height = DIAG // 2
-    x, z = lax.div(rows.me, WIDTH), lax.rem(rows.me, WIDTH)
+    x, z = rows.major_me, rows.minor_me
+    sent = []
 
     def at(half, near, far):
         first, second = (z, x) if half == 0 else (x, z)
         first, second = lax.rem(first + near, WIDTH), lax.rem(second + far, WIDTH)
         return second * WIDTH + first if half == 0 else first * WIDTH + second
 
-    def block(half, device):
-        return row_out.at[pl.ds(pl.multiple_of(device * DIAG + half * height, 8), height)]
-
-    def row_copy(half, source, sems, device):
-        there = block(half, source[1])
+    def region(out, device, offset, size):
+        return out.at[pl.ds(pl.multiple_of(device * DIAG + offset, 8), size)]
+
+    def remote(src, dst, sems, index, axis, device):
         return pltpu.make_async_remote_copy(
-            src_ref=source[0],
-            dst_ref=there,
-            send_sem=sems[0],
-            recv_sem=sems[1],
-            device_id={"col": device},
+            src_ref=src,
+            dst_ref=dst,
+            send_sem=sems.at[(0, *index)],
+            recv_sem=sems.at[(1, *index)],
+            device_id={axis: device},
             device_id_type=MESH,
         )
 
-    def near_copy(half, d, device, owner):
-        sems = near_sems.at[0, half, d], near_sems.at[1, half, d]
-        return row_copy(half, (rows.fin.at[pl.ds(half * height, height)], owner), sems, device)
-
-    def far_copy(half, e, d, device, owner):
-        sems = far_sems.at[0, half, e, d], far_sems.at[1, half, e, d]
-        source = rows.fin.at[pl.ds(half * height, height)] if e == 0 else block(half, owner)
-        return row_copy(half, (source, owner), sems, device)
-
+    def row_region(half, owner, part):
+        if part is None:
+            return region(row_out, owner, half * height, height)
+        return region(row_out, owner, half * height + part * (height // 2), height // 2)
+
+    def row_send(half, owner, part, sems, index, device, src=None):
+        dst = row_region(half, owner, part)
+        copy = remote(dst if src is None else src, dst, sems, index, "col", device)
+        copy.start()
+        sent.append(copy)
+
+    def row_wait(half, owner, part, sems, index, device):
+        there = row_region(half, owner, part)
+        remote(there, there, sems, index, "col", device).wait_recv()
+
+    def far_send(half, e, owner, src=None):
+        for way, far in enumerate((1, 3)):
+            row_send(half, owner, None, far_sems, (half, e, 0, way), at(half, 0, far), src)
+
+    def far_pass(half, e, near):
+        for way, (far, on) in enumerate(((3, 1), (1, 3))):
+            owner = at(half, near, far)
+            row_wait(half, owner, None, far_sems, (half, e, 0, way), at(half, 0, far))
+            row_send(half, owner, way, far_sems, (half, e, 1, way), at(half, 0, on))
+
+    def col_region(owner, part):
+        if part is None:
+            return region(col_out, owner, 0, DIAG)
+        return region(col_out, owner, part * height, height)
+
+    def col_send(owner, part, sems, index, device, src=None):
+        dst = col_region(owner, part)
+        copy = remote(dst if src is None else src, dst, sems, index, "row", device)
+        copy.start()
+        sent.append(copy)
+
+    def col_wait(owner, part, sems, index, device):
+        there = col_region(owner, part)
+        remote(there, there, sems, index, "row", device).wait_recv()
+
+    other = cols.shifted(0, 1)
     rows.fin[...] = rows.own[...]
-    for d in range(1, WIDTH):
-        for half in range(2):
-            near_copy(half, d, at(half, d, 0), rows.me).start()
+    mine = [rows.fin.at[pl.ds(half * height, height)] for half in range(2)]
+    for half in range(2):
+        for way, near in enumerate((1, 3)):
+            row_send(half, rows.me, None, near_sems, (half, 0, way), at(half, near, 0), mine[half])
     cols.fin[...] = cols.own[...]
-    col_place = col_out.at[pl.ds(pl.multiple_of(cols.me * DIAG, DIAG), DIAG)]
-    for d in range(1, cols.count):
-        cols.copy(LAST(), d, cols.fin, col_place, cols.partner(d)).start()
-    for d in range(1, WIDTH):
-        for half in range(2):
-            far_copy(half, 0, d, at(half, 0, d), rows.me).start()
-    row_place = row_out.at[pl.ds(pl.multiple_of(rows.me * DIAG, DIAG), DIAG)]
+    for way, step in enumerate((1, 3)):
+        col_send(cols.me, None, ring_sems, (0, way), cols.shifted(step, 0), cols.fin)
+    for half in range(2):
+        far_send(half, 0, rows.me, mine[half])
+    col_send(cols.me, None, core_sems, (0,), other, cols.fin)
     kept = (
-        pltpu.make_async_copy(rows.fin, row_place, out_sems.at[0]),
-        pltpu.make_async_copy(cols.fin, col_place, out_sems.at[1]),
+        pltpu.make_async_copy(rows.fin, region(row_out, rows.me, 0, DIAG), out_sems.at[0]),
+        pltpu.make_async_copy(cols.fin, region(col_out, cols.me, 0, DIAG), out_sems.at[1]),
     )
     for copy in kept:
         copy.start()
     flag_out[0, 0] = jnp.max(cols.told(all_flags)).astype(jnp.int32)
+    ways = ((3, 1), (1, 3))
+    for way, (near, on) in enumerate(ways):
+        for half in range(2):
+            owner = at(half, near, 0)
+            row_wait(half, owner, None, near_sems, (half, 0, way), owner)
+            row_send(half, owner, way, near_sems, (half, 1, way), at(half, on, 0))
+            far_send(half, 1 + way, owner)
+        owner = cols.shifted(near, 0)
+        col_wait(owner, None, ring_sems, (0, way), owner)
+        col_send(owner, way, ring_sems, (1, way), cols.shifted(on, 0))
+        col_send(owner, None, core_sems, (1 + way,), other)
+    for half in range(2):
+        far_pass(half, 0, 0)
+    for half in range(2):
+        owner = at(half, 2, 0)
+        for way, (near, on) in enumerate(ways):
+            row_wait(half, owner, way, near_sems, (half, 1, way), at(half, near, 0))
+        far_send(half, 3, owner)
+    owner = cols.shifted(2, 0)
+    for way, (near, on) in enumerate(ways):
+        col_wait(owner, way, ring_sems, (1, way), cols.shifted(near, 0))
+    col_send(owner, None, core_sems, (3,), other)
+    nears = (0, 3, 1, 2)
     for e in range(1, WIDTH):
         for half in range(2):
-            owner = at(half, WIDTH - e, 0)
-            near_copy(half, e, owner, owner).wait_recv()
-            for d in range(1, WIDTH):
-                far_copy(half, e, d, at(half, 0, d), owner).start()
-    for d in range(1, WIDTH):
+            far_pass(half, e, nears[e])
+    for e in range(WIDTH):
         for half in range(2):
-            for e in range(WIDTH):
-                sender = at(half, 0, WIDTH - d)
-                far_copy(half, e, d, sender, at(half, WIDTH - e, WIDTH - d)).wait_recv()
-    for d in range(1, cols.count):
-        peer = cols.sender(d)
-        there = col_out.at[pl.ds(pl.multiple_of(peer * DIAG, DIAG), DIAG)]
-        cols.copy(LAST(), d, cols.fin, there, peer).wait_recv()
-        cols.copy(LAST(), d, cols.fin, col_place, cols.partner(d)).wait_send()
-    for d in range(1, WIDTH):
-        for half in range(2):
-            near_copy(half, d, at(half, d, 0), rows.me).wait_send()
-            for e in range(WIDTH):
-                owner = at(half, WIDTH - e, 0) if e else rows.me
-                far_copy(half, e, d, at(half, 0, d), owner).wait_send()
+            for way, (far, on) in enumerate(ways):
+                row_wait(half, at(half, nears[e], 2), way, far_sems, (half, e, 1, way), at(half, 0, far))
+        col_wait(cols.shifted(nears[e], 1), None, core_sems, (e,), other)
+    for copy in sent:
+        copy.wait_send()
     for copy in kept:
         copy.wait()
 
@@ -615,8 +655,10 @@
             pltpu.VMEM((8, TILE), f32),
             pltpu.SemaphoreType.DMA((3, max(PARTS))),
             pltpu.SemaphoreType.DMA((2,)),
-            pltpu.SemaphoreType.DMA((2, 2, WIDTH)),
-            pltpu.SemaphoreType.DMA((2, 2, WIDTH, WIDTH)),
+            pltpu.SemaphoreType.DMA((2, 2, 2, 2)),
+            pltpu.SemaphoreType.DMA((2, 2, WIDTH, 2, 2)),
+            pltpu.SemaphoreType.DMA((2, 2, 2)),
+            pltpu.SemaphoreType.DMA((2, WIDTH)),
             *side_scratch(n_col, ROW_CAP, TAIL, TAIL),
             *side_scratch(n_row, COL_CAP, TILE, TILE),
         ],

time: 86.5 us -> 91.9 us (1.062)
  Pallas kernels: 84.1 us -> 89.6 us
    pallas_call x1, Pallas kernels: 82.9 us -> 88.3 us  [sparse(): pl.pallas_call(functools.partial(kernel, n_row, n_col), out_shape=(jax.Sh...]
where the time goes in v5:
time: 91.9 us; the launch traced here: 91.8 us
  Pallas kernels  89.6 us (97%)
  between operations  2.18 us (2%)
    pallas_call x1, Pallas kernels, sparse(): pl.pallas_call(functools.partial(kernel, n_row, n_col), out_shape=(jax.Sh...  88.3 us

profile of v5, /device:TPU:0, one launch (start us, length us, event | category | flops | bytes accessed | tf_op | source)
XLA Modules:
  0.0 91.8 jit_solution(8818277996061077227)
XLA Ops:
  0.6 0.0 copy-start.5
  0.6 0.0 copy-start.4
  1.3 88.3 %shard_map.59 = (f32[2048,128]{1,0:T(8,128)S(1)}, f32[1024,128]{1,0:T(8,128)S(1)}, s32[1,1]{1,0:T(1,128)}) custom-call(s32[1,1]{1,0:T(1,128)S(6)} %copy.45.count_ref, s32[1,288]{1,0:T(1,128)} %bitcast.45, s32[1,288]{1,0:T(1,128)} %bitcast.46, f32[288,128,128]{2,1,0:T(8,128)} %bitcast.43), custom_call_target="tpu_custom_call" | custom-call | tf_op jit(solution)/shard_map/pallas_call | solution.py:630
  90.3 0.0 copy-done.5
  90.4 0.0 copy-done.4
  90.4 1.3 %conditional.2 = (f32[262144]{0:T(1024)}, f32[131072]{0:T(1024)}) conditional(s32[]{:T(128)} %bitcast.12, (f32[2048,128]{1,0:T(8,128)S(1)}, f32[1024,128]{1,0:T(8,128)S(1)}) %tuple.113, (s32[1,1,288]{2,1,0:T(1,128)S(1)}, s32[1,1]{1,0:T(1,128)}, f32[288,128,128]{2,1,0:T(8,128)}, s32[1,1,288]{2,1,0:T(1,128)S(1)}) %tuple.203), branch_computations={%region_0.0_spmd, %region_1.26_spmd} | conditional | flops 40769284 | bytes 240286992 | solution.py:750
  90.4 1.2 %branch_0_fun.1 = (f32[2048,128]{1,0:T(8,128)}, f32[1024,128]{1,0:T(8,128)}) custom-call(f32[2048,128]{1,0:T(8,128)S(1)} %get-tuple-element.436.row_ref, f32[1024,128]{1,0:T(8,128)S(1)} %get-tuple-element.437.col_ref), custom_call_target="tpu_custom_call" | custom-call | tf_op jit(solution)/shard_map/cond/branch_0_fun/pallas_call | solution.py:686
Async XLA Ops:
  0.6 89.7 %copy-start.5 = (s32[1,1,288]{2,1,0:T(1,128)S(1)}, s32[1,1,288]{2,1,0:T(1,128)}, u32[]{:S(2)}) copy-start(s32[1,1,288]{2,1,0:T(1,128)} %param.24) | copy-start | bytes 3460
  0.6 89.7 %copy-start.4 = (s32[1,1,288]{2,1,0:T(1,128)S(1)}, s32[1,1,288]{2,1,0:T(1,128)}, u32[]{:S(2)}) copy-start(s32[1,1,288]{2,1,0:T(1,128)} %param.23) | copy-start | bytes 3460

commit v6 on v4

--- a/solution.py
+++ b/solution.py
@@ -111,17 +111,13 @@
         a, b = self.steps[d - 1]
         return self.shifted(a, b)
 
-    def sender(self, d):
-        a, b = self.steps[d - 1]
-        return self.shifted(WIDTH - a, self.minor - b)
-
-    def copy(self, kind, d, src, dst, peer):
+    def copy(self, kind, src, dst, peer):
         kind, slot = kind
         return pltpu.make_async_remote_copy(
             src_ref=src,
             dst_ref=dst,
-            send_sem=self.send_sems.at[kind, d],
-            recv_sem=self.recv_sems.at[kind, slot, d],
+            send_sem=self.send_sems.at[kind],
+            recv_sem=self.recv_sems.at[kind, slot],
             device_id={self.axis: peer},
             device_id_type=MESH,
         )
@@ -132,29 +128,27 @@
     def send(self, kind, send, recv):
         for d in range(1, self.count):
             peer = self.partner(d)
-            self.copy(kind, d, self.place(send, peer), self.place(recv, self.me), peer).start()
+            self.copy(kind, self.place(send, peer), self.place(recv, self.me), peer).start()
         self.place(recv, self.me)[...] = self.place(send, self.me)[...]
 
-    def wait_send(self, kind, send, recv):
-        for d in range(1, self.count):
-            peer = self.partner(d)
-            self.copy(kind, d, self.place(send, peer), self.place(recv, self.me), peer).wait_send()
-
-    def wait_recv(self, kind, send, recv):
-        for d in range(1, self.count):
-            peer = self.sender(d)
-            self.copy(kind, d, self.place(send, peer), self.place(recv, peer), peer).wait_recv()
+    def wait(self, sem, ref, size):
+        whole = ref.at[pl.ds(0, size)]
+        pltpu.make_async_copy(whole, whole, sem).wait()
+
+    def wait_send(self, kind, send):
+        self.wait(self.send_sems.at[kind[0]], send, (self.count - 1) * self.cap)
+
+    def wait_recv(self, kind, recv):
+        self.wait(self.recv_sems.at[kind[0], kind[1]], recv, (self.count - 1) * self.cap)
 
     def tell(self, flag_ref):
         for d in range(1, self.count):
-            self.copy((4, 0), d, flag_ref, self.flags.at[self.me], self.partner(d)).start()
+            self.copy((4, 0), flag_ref, self.flags.at[self.me], self.partner(d)).start()
         self.flags[self.me] = flag_ref[...]
 
-    def told(self, flag_ref):
-        for d in range(1, self.count):
-            peer = self.sender(d)
-            self.copy((4, 0), d, flag_ref, self.flags.at[peer], peer).wait_recv()
-            self.copy((4, 0), d, flag_ref, self.flags.at[self.me], self.partner(d)).wait_send()
+    def told(self):
+        self.wait(self.recv_sems.at[4, 0], self.flags, self.count - 1)
+        self.wait(self.send_sems.at[4], self.flags, self.count - 1)
         return jnp.max(self.flags[...], axis=0)
 
 
@@ -233,12 +227,12 @@
 
 
 def put_done(side, slot):
-    side.wait_send(FIRST(slot), side.p1_send, side.p1_recv.at[slot])
+    side.wait_send(FIRST(slot), side.p1_send)
 
 
 def combine(side, slot, final):
     recv = side.p1_recv.at[slot]
-    side.wait_recv(FIRST(slot), side.p1_send, recv)
+    side.wait_recv(FIRST(slot), recv)
     terms = select_rows(side.levels[...], recv[...])
     terms = terms.reshape(LEVELS, TILE, TILE)
     if final:
@@ -258,7 +252,7 @@
 
 def take_back(side, slot):
     recv = side.p2_recv.at[slot]
-    side.wait_recv(BACK(slot), side.p2_send, recv)
+    side.wait_recv(BACK(slot), recv)
     scale = select_rows(side.unpack[...], recv[...])
     side.ext[...] = scale[:TILE].T
     tail = scale[TILE : TILE + TAIL]
@@ -267,7 +261,7 @@
         side.tail[...] = jnp.concatenate(tail, axis=0).T[:TAIL]
     else:
         side.tail[...] = jnp.concatenate([tail] * QUARTERS, axis=0).T
-    side.wait_send(BACK(slot), side.p2_send, recv)
+    side.wait_send(BACK(slot), side.p2_send)
 
 
 def gather_terms(side, final):
@@ -431,14 +425,14 @@
         side.own[...] = jnp.ones_like(side.own)
     first_pass(0, ext_tiles, ext_half, rows.ext_turned, cols.ext_turned)
     first_tail()
-    for side in sides:
-        side.wait_send(ID(), side.p1_send, side.id_recv)
+    for side in (rows, cols):
+        side.wait_send(ID(), side.p1_send)
         gather_terms(side, False)
         fill(side)
         put(side, 0)
     first_pass(2, diag_tiles, 0.5, rows.diag_term, cols.diag_term)
     for side in sides:
-        side.wait_recv(ID(), side.p1_send, side.id_recv)
+        side.wait_recv(ID(), side.id_recv)
         learn(side, flag_ref)
     rows.tell(flag_ref)
     for side in sides:
@@ -478,7 +472,7 @@
 
     for t in range(1, SWEEPS):
         sweep(t, False)
-    all_flags[...] = rows.told(flag_ref)
+    all_flags[...] = rows.told()
     cols.tell(all_flags)
     sweep(SWEEPS, True)
 
@@ -520,7 +514,7 @@
     cols.fin[...] = cols.own[...]
     col_place = col_out.at[pl.ds(pl.multiple_of(cols.me * DIAG, DIAG), DIAG)]
     for d in range(1, cols.count):
-        cols.copy(LAST(), d, cols.fin, col_place, cols.partner(d)).start()
+        cols.copy(LAST(), cols.fin, col_place, cols.partner(d)).start()
     for d in range(1, WIDTH):
         for half in range(2):
             far_copy(half, 0, d, at(half, 0, d), rows.me).start()
@@ -531,7 +525,7 @@
     )
     for copy in kept:
         copy.start()
-    flag_out[0, 0] = jnp.max(cols.told(all_flags)).astype(jnp.int32)
+    flag_out[0, 0] = jnp.max(cols.told()).astype(jnp.int32)
     for e in range(1, WIDTH):
         for half in range(2):
             owner = at(half, WIDTH - e, 0)
@@ -543,11 +537,8 @@
             for e in range(WIDTH):
                 sender = at(half, 0, WIDTH - d)
                 far_copy(half, e, d, sender, at(half, WIDTH - e, WIDTH - d)).wait_recv()
-    for d in range(1, cols.count):
-        peer = cols.sender(d)
-        there = col_out.at[pl.ds(pl.multiple_of(peer * DIAG, DIAG), DIAG)]
-        cols.copy(LAST(), d, cols.fin, there, peer).wait_recv()
-        cols.copy(LAST(), d, cols.fin, col_place, cols.partner(d)).wait_send()
+    cols.wait(cols.recv_sems.at[3, 0], col_out, (cols.count - 1) * DIAG)
+    cols.wait(cols.send_sems.at[3], col_out, (cols.count - 1) * DIAG)
     for d in range(1, WIDTH):
         for half in range(2):
             near_copy(half, d, at(half, d, 0), rows.me).wait_send()
@@ -580,8 +571,8 @@
         pltpu.VMEM((2, entries, TILE), f32),
         pltpu.VMEM((DIAG, TILE), f32),
         pltpu.VMEM((count, 8, TILE), f32),
-        pltpu.SemaphoreType.DMA((5, count)),
-        pltpu.SemaphoreType.DMA((5, 2, count)),
+        pltpu.SemaphoreType.DMA((5,)),
+        pltpu.SemaphoreType.DMA((5, 2)),
     ]
 
 

time: 86.5 us -> 83.5 us (0.965)
  Pallas kernels: 84.1 us -> 80.9 us
    pallas_call x1, Pallas kernels: 82.9 us -> 79.7 us  [sparse(): pl.pallas_call(functools.partial(kernel, n_row, n_col), out_shape=(jax.Sh...]
where the time goes in v6:
time: 83.5 us; the launch traced here: 83.3 us
  Pallas kernels  80.9 us (97%)
  between operations  2.2 us (3%)
    pallas_call x1, Pallas kernels, sparse(): pl.pallas_call(functools.partial(kernel, n_row, n_col), out_shape=(jax.Sh...  79.7 us

profile of v6, /device:TPU:0, one launch (start us, length us, event | category | flops | bytes accessed | tf_op | source)
XLA Modules:
  0.0 83.3 jit_solution(15251430468904111030)
XLA Ops:
  0.6 0.0 copy-start.5
  0.6 0.0 copy-start.4
  1.3 79.7 %shard_map.59 = (f32[2048,128]{1,0:T(8,128)S(1)}, f32[1024,128]{1,0:T(8,128)S(1)}, s32[1,1]{1,0:T(1,128)}) custom-call(s32[1,1]{1,0:T(1,128)S(6)} %copy.45.count_ref, s32[1,288]{1,0:T(1,128)} %bitcast.45, s32[1,288]{1,0:T(1,128)} %bitcast.46, f32[288,128,128]{2,1,0:T(8,128)} %bitcast.43), custom_call_target="tpu_custom_call" | custom-call | tf_op jit(solution)/shard_map/pallas_call | solution.py:581
  81.7 0.0 copy-done.5
  81.7 0.0 copy-done.4
  81.7 1.5 %conditional.2 = (f32[262144]{0:T(1024)}, f32[131072]{0:T(1024)}) conditional(s32[]{:T(128)} %bitcast.12, (f32[2048,128]{1,0:T(8,128)S(1)}, f32[1024,128]{1,0:T(8,128)S(1)}) %tuple.113, (s32[1,1,288]{2,1,0:T(1,128)S(1)}, s32[1,1]{1,0:T(1,128)}, f32[288,128,128]{2,1,0:T(8,128)}, s32[1,1,288]{2,1,0:T(1,128)S(1)}) %tuple.203), branch_computations={%region_0.0_spmd, %region_1.26_spmd} | conditional | flops 40769284 | bytes 240286992 | solution.py:699
  81.7 1.2 %branch_0_fun.1 = (f32[2048,128]{1,0:T(8,128)}, f32[1024,128]{1,0:T(8,128)}) custom-call(f32[2048,128]{1,0:T(8,128)S(1)} %get-tuple-element.436.row_ref, f32[1024,128]{1,0:T(8,128)S(1)} %get-tuple-element.437.col_ref), custom_call_target="tpu_custom_call" | custom-call | tf_op jit(solution)/shard_map/cond/branch_0_fun/pallas_call | solution.py:635
Async XLA Ops:
  0.6 81.0 %copy-start.5 = (s32[1,1,288]{2,1,0:T(1,128)S(1)}, s32[1,1,288]{2,1,0:T(1,128)}, u32[]{:S(2)}) copy-start(s32[1,1,288]{2,1,0:T(1,128)} %param.24) | copy-start | bytes 3460
  0.6 81.0 %copy-start.4 = (s32[1,1,288]{2,1,0:T(1,128)S(1)}, s32[1,1,288]{2,1,0:T(1,128)}, u32[]{:S(2)}) copy-start(s32[1,1,288]{2,1,0:T(1,128)} %param.23) | copy-start | bytes 3460

commit v7 on v6

--- a/solution.py
+++ b/solution.py
@@ -324,7 +324,7 @@
     load_sems,
     out_sems,
     near_sems,
-    far_sems,
+    far_sem,
     *rest,
 ):
     rows = Side("col", n_col, ROW_CAP, 0, rest[: len(rest) // 2])
@@ -456,6 +456,15 @@
         fill(cols)
         put(cols, slot)
 
+    col_place = col_out.at[pl.ds(pl.multiple_of(cols.me * DIAG, DIAG), DIAG)]
+    kept_columns = pltpu.make_async_copy(cols.fin, col_place, out_sems.at[1])
+
+    def spread_columns():
+        cols.fin[...] = cols.own[...]
+        for d in range(1, cols.count):
+            cols.copy(LAST(), cols.fin, col_place, cols.partner(d)).start()
+        kept_columns.start()
+
     def sweep(t, final):
         slot, before = t % 2, (t + 1) % 2
         first, second = (row_step, col_step) if t % 2 else (col_step, row_step)
@@ -467,6 +476,8 @@
             combine(side, slot, final)
             if not final:
                 give_back(side, slot)
+            elif side is cols:
+                spread_columns()
         for side in sides:
             put_done(side, slot)
 
@@ -499,11 +510,11 @@
         )
 
     def near_copy(half, d, device, owner):
-        sems = near_sems.at[0, half, d], near_sems.at[1, half, d]
+        sems = rows.send_sems.at[3], near_sems.at[half, d]
         return row_copy(half, (rows.fin.at[pl.ds(half * height, height)], owner), sems, device)
 
     def far_copy(half, e, d, device, owner):
-        sems = far_sems.at[0, half, e, d], far_sems.at[1, half, e, d]
+        sems = rows.send_sems.at[3], far_sem.at[0]
         source = rows.fin.at[pl.ds(half * height, height)] if e == 0 else block(half, owner)
         return row_copy(half, (source, owner), sems, device)
 
@@ -511,20 +522,12 @@
     for d in range(1, WIDTH):
         for half in range(2):
             near_copy(half, d, at(half, d, 0), rows.me).start()
-    cols.fin[...] = cols.own[...]
-    col_place = col_out.at[pl.ds(pl.multiple_of(cols.me * DIAG, DIAG), DIAG)]
-    for d in range(1, cols.count):
-        cols.copy(LAST(), cols.fin, col_place, cols.partner(d)).start()
     for d in range(1, WIDTH):
         for half in range(2):
             far_copy(half, 0, d, at(half, 0, d), rows.me).start()
     row_place = row_out.at[pl.ds(pl.multiple_of(rows.me * DIAG, DIAG), DIAG)]
-    kept = (
-        pltpu.make_async_copy(rows.fin, row_place, out_sems.at[0]),
-        pltpu.make_async_copy(cols.fin, col_place, out_sems.at[1]),
-    )
-    for copy in kept:
-        copy.start()
+    kept_rows = pltpu.make_async_copy(rows.fin, row_place, out_sems.at[0])
+    kept_rows.start()
     flag_out[0, 0] = jnp.max(cols.told()).astype(jnp.int32)
     for e in range(1, WIDTH):
         for half in range(2):
@@ -532,21 +535,13 @@
             near_copy(half, e, owner, owner).wait_recv()
             for d in range(1, WIDTH):
                 far_copy(half, e, d, at(half, 0, d), owner).start()
-    for d in range(1, WIDTH):
-        for half in range(2):
-            for e in range(WIDTH):
-                sender = at(half, 0, WIDTH - d)
-                far_copy(half, e, d, sender, at(half, WIDTH - e, WIDTH - d)).wait_recv()
+    far_count, near_count = 2 * WIDTH * (WIDTH - 1), 2 * (WIDTH - 1)
+    rows.wait(far_sem.at[0], row_out, far_count * height)
     cols.wait(cols.recv_sems.at[3, 0], col_out, (cols.count - 1) * DIAG)
     cols.wait(cols.send_sems.at[3], col_out, (cols.count - 1) * DIAG)
-    for d in range(1, WIDTH):
-        for half in range(2):
-            near_copy(half, d, at(half, d, 0), rows.me).wait_send()
-            for e in range(WIDTH):
-                owner = at(half, WIDTH - e, 0) if e else rows.me
-                far_copy(half, e, d, at(half, 0, d), owner).wait_send()
-    for copy in kept:
-        copy.wait()
+    rows.wait(rows.send_sems.at[3], row_out, (far_count + near_count) * height)
+    kept_rows.wait()
+    kept_columns.wait()
 
 
 def side_scratch(count, cap, tail_scale, tail_term):
@@ -606,8 +601,8 @@
             pltpu.VMEM((8, TILE), f32),
             pltpu.SemaphoreType.DMA((3, max(PARTS))),
             pltpu.SemaphoreType.DMA((2,)),
-            pltpu.SemaphoreType.DMA((2, 2, WIDTH)),
-            pltpu.SemaphoreType.DMA((2, 2, WIDTH, WIDTH)),
+            pltpu.SemaphoreType.DMA((2, WIDTH)),
+            pltpu.SemaphoreType.DMA((1,)),
             *side_scratch(n_col, ROW_CAP, TAIL, TAIL),
             *side_scratch(n_row, COL_CAP, TILE, TILE),
         ],

time: 83.5 us -> 82.6 us (0.989)
  Pallas kernels: 80.9 us -> 80 us
    pallas_call x1, Pallas kernels: 79.7 us -> 78.8 us  [sparse(): pl.pallas_call(functools.partial(kernel, n_row, n_col), out_shape=(jax.Sh...]
where the time goes in v7:
time: 82.6 us; the launch traced here: 82.5 us
  Pallas kernels  80 us (97%)
  between operations  2.2 us (3%)
    pallas_call x1, Pallas kernels, sparse(): pl.pallas_call(functools.partial(kernel, n_row, n_col), out_shape=(jax.Sh...  78.8 us

profile of v7, /device:TPU:0, one launch (start us, length us, event | category | flops | bytes accessed | tf_op | source)
XLA Modules:
  0.0 82.5 jit_solution(15301678674331595790)
XLA Ops:
  0.6 0.0 copy-start.5
  0.6 0.0 copy-start.4
  1.3 78.8 %shard_map.59 = (f32[2048,128]{1,0:T(8,128)S(1)}, f32[1024,128]{1,0:T(8,128)S(1)}, s32[1,1]{1,0:T(1,128)}) custom-call(s32[1,1]{1,0:T(1,128)S(6)} %copy.45.count_ref, s32[1,288]{1,0:T(1,128)} %bitcast.45, s32[1,288]{1,0:T(1,128)} %bitcast.46, f32[288,128,128]{2,1,0:T(8,128)} %bitcast.43), custom_call_target="tpu_custom_call" | custom-call | tf_op jit(solution)/shard_map/pallas_call | solution.py:576
  80.8 0.0 copy-done.5
  80.8 0.0 copy-done.4
  80.8 1.5 %conditional.2 = (f32[262144]{0:T(1024)}, f32[131072]{0:T(1024)}) conditional(s32[]{:T(128)} %bitcast.12, (f32[2048,128]{1,0:T(8,128)S(1)}, f32[1024,128]{1,0:T(8,128)S(1)}) %tuple.113, (s32[1,1,288]{2,1,0:T(1,128)S(1)}, s32[1,1]{1,0:T(1,128)}, f32[288,128,128]{2,1,0:T(8,128)}, s32[1,1,288]{2,1,0:T(1,128)S(1)}) %tuple.203), branch_computations={%region_0.0_spmd, %region_1.26_spmd} | conditional | flops 40769284 | bytes 240286992 | solution.py:694
  80.8 1.2 %branch_0_fun.1 = (f32[2048,128]{1,0:T(8,128)}, f32[1024,128]{1,0:T(8,128)}) custom-call(f32[2048,128]{1,0:T(8,128)S(1)} %get-tuple-element.436.row_ref, f32[1024,128]{1,0:T(8,128)S(1)} %get-tuple-element.437.col_ref), custom_call_target="tpu_custom_call" | custom-call | tf_op jit(solution)/shard_map/cond/branch_0_fun/pallas_call | solution.py:630
Async XLA Ops:
  0.6 80.2 %copy-start.5 = (s32[1,1,288]{2,1,0:T(1,128)S(1)}, s32[1,1,288]{2,1,0:T(1,128)}, u32[]{:S(2)}) copy-start(s32[1,1,288]{2,1,0:T(1,128)} %param.24) | copy-start | bytes 3460
  0.6 80.2 %copy-start.4 = (s32[1,1,288]{2,1,0:T(1,128)S(1)}, s32[1,1,288]{2,1,0:T(1,128)}, u32[]{:S(2)}) copy-start(s32[1,1,288]{2,1,0:T(1,128)} %param.23) | copy-start | bytes 3460

commit v8 on v7

--- a/solution.py
+++ b/solution.py
@@ -469,8 +469,11 @@
         slot, before = t % 2, (t + 1) % 2
         first, second = (row_step, col_step) if t % 2 else (col_step, row_step)
         first(slot, before, final)
+        if t % 2:
+            row_pass(diag_tiles, cols.own_turned, rows.diag_term, final)
         second(slot, before, final)
-        row_pass(diag_tiles, cols.own_turned, rows.diag_term, final)
+        if t % 2 == 0:
+            row_pass(diag_tiles, cols.own_turned, rows.diag_term, final)
         col_pass(diag_tiles, rows.own_turned, cols.diag_term, final)
         for side in (rows, cols) if t % 2 else (cols, rows):
             combine(side, slot, final)

time: 82.6 us -> 82.6 us (level)
  no operation moved by 1% of the time
where the time goes in v8:
time: 82.6 us; the launch traced here: 82.5 us
  Pallas kernels  80 us (97%)
  between operations  2.2 us (3%)
    pallas_call x1, Pallas kernels, sparse(): pl.pallas_call(functools.partial(kernel, n_row, n_col), out_shape=(jax.Sh...  78.8 us

profile of v8, /device:TPU:0, one launch (start us, length us, event | category | flops | bytes accessed | tf_op | source)
XLA Modules:
  0.0 82.5 jit_solution(12010683080064425606)
XLA Ops:
  0.6 0.0 copy-start.5
  0.6 0.0 copy-start.4
  1.3 78.8 %shard_map.59 = (f32[2048,128]{1,0:T(8,128)S(1)}, f32[1024,128]{1,0:T(8,128)S(1)}, s32[1,1]{1,0:T(1,128)}) custom-call(s32[1,1]{1,0:T(1,128)S(6)} %copy.45.count_ref, s32[1,288]{1,0:T(1,128)} %bitcast.45, s32[1,288]{1,0:T(1,128)} %bitcast.46, f32[288,128,128]{2,1,0:T(8,128)} %bitcast.43), custom_call_target="tpu_custom_call" | custom-call | tf_op jit(solution)/shard_map/pallas_call | solution.py:579
  80.8 0.0 copy-done.5
  80.8 0.0 copy-done.4
  80.8 1.5 %conditional.2 = (f32[262144]{0:T(1024)}, f32[131072]{0:T(1024)}) conditional(s32[]{:T(128)} %bitcast.12, (f32[2048,128]{1,0:T(8,128)S(1)}, f32[1024,128]{1,0:T(8,128)S(1)}) %tuple.113, (s32[1,1,288]{2,1,0:T(1,128)S(1)}, s32[1,1]{1,0:T(1,128)}, f32[288,128,128]{2,1,0:T(8,128)}, s32[1,1,288]{2,1,0:T(1,128)S(1)}) %tuple.203), branch_computations={%region_0.0_spmd, %region_1.26_spmd} | conditional | flops 40769284 | bytes 240286992 | solution.py:697
  80.8 1.2 %branch_0_fun.1 = (f32[2048,128]{1,0:T(8,128)}, f32[1024,128]{1,0:T(8,128)}) custom-call(f32[2048,128]{1,0:T(8,128)S(1)} %get-tuple-element.436.row_ref, f32[1024,128]{1,0:T(8,128)S(1)} %get-tuple-element.437.col_ref), custom_call_target="tpu_custom_call" | custom-call | tf_op jit(solution)/shard_map/cond/branch_0_fun/pallas_call | solution.py:633
Async XLA Ops:
  0.6 80.2 %copy-start.5 = (s32[1,1,288]{2,1,0:T(1,128)S(1)}, s32[1,1,288]{2,1,0:T(1,128)}, u32[]{:S(2)}) copy-start(s32[1,1,288]{2,1,0:T(1,128)} %param.24) | copy-start | bytes 3460
  0.6 80.2 %copy-start.4 = (s32[1,1,288]{2,1,0:T(1,128)S(1)}, s32[1,1,288]{2,1,0:T(1,128)}, u32[]{:S(2)}) copy-start(s32[1,1,288]{2,1,0:T(1,128)} %param.23) | copy-start | bytes 3460
